TPU v7x, 512 devices: a whole 4x8x8 slice. The times are simulated.
512 devices in a mesh: gx: 32 (over y, x), gy: 16 (over z, core).
Axes of the slice: x: 4, y: 8, z: 8, core: 2. Of those that a mesh axis runs over, the one named last changes fastest.
Arguments:
- water_head: float32 [1024, 512, 128], P('gx', 'gy'), may hold values from -4 to 4
- conductivity: float32 [1024, 512, 128], P('gx', 'gy'), may hold values from 1 to 8
- recharge: float32 [1024, 512, 128], P('gx', 'gy'), may hold values from -4 to 4
Outputs:
- next_head: float32 [1024, 512, 128], P('gx', 'gy')
All inputs are finite; a program needn't handle non-finite values.
Results may differ from a plain program's by a relative error of at most 0.008.
Values sent between devices are 32-bit elements; how exact they have to be, the bound alone decides.
No kernel may reach another device: no remote copies, remote signals or barrier semaphores. Data moves between devices by JAX's collectives and lax.ppermute only.
A program may use at most 64 MiB of HBM per device.

v0:
```python
import functools

import jax
import jax.numpy as jnp
from jax import lax
from jax.experimental import pallas as pl
from jax.experimental.pallas import tpu as pltpu
from jax.sharding import PartitionSpec as P

COEF_Z = 8.0
COEF_X = 5120.0
COEF_Y = 5120.0

N = 32
L = 128
ROWS = N * N


def link(coef, one, other):
    return coef * (one * other) / (one + other)


def xp(i):
    return pl.ds(pl.multiple_of(i * N, N), N)


def yp(j):
    return pl.ds(j, N, stride=N)


def pack_kernel(h, k, xlo, xhi, ylo, yhi):
    for out, at in ((xlo, xp(0)), (xhi, xp(N - 1)), (ylo, yp(0)), (yhi, yp(N - 1))):
        out[0] = h[at, :]
        out[1] = k[at, :]


def factor_kernel(h, k, rc, f, bx, ex, ix, mx, by, ey, iy, my, ez, iz, wx, wy, wz, wzt):
    def y_links(j, carry):
        k0, h0, low = carry
        k1, h1 = k[yp(j), :], h[yp(j), :]
        w = link(COEF_Y, k0, k1)
        wy[xp(j), :] = w
        up = 2.0 * w * (h1 - h0)
        f[yp(j - 1), :] = up - low
        return k1, h1, up

    _, _, low = lax.fori_loop(
        1, N, y_links, (k[yp(0), :], h[yp(0), :], jnp.zeros((N, L), jnp.float32)), unroll=4
    )
    f[yp(N - 1), :] = -low

    lane = lax.broadcasted_iota(jnp.int32, (N, L), 1)

    def z_part(kk, hh):
        ku = pltpu.roll(kk, L - 1, 1)
        hu = pltpu.roll(hh, L - 1, 1)
        w = jnp.where(lane < L - 1, link(COEF_Z, kk, ku), 0.0)
        up = 2.0 * w * (hu - hh)
        return w, up - pltpu.roll(up, 1, 1)

    def x_links(i, carry):
        k0, h0, low = carry
        k1, h1 = k[xp(i), :], h[xp(i), :]
        w = link(COEF_X, k0, k1)
        wx[xp(i), :] = w
        up = 2.0 * w * (h1 - h0)
        wzi, fz = z_part(k0, h0)
        wz[xp(i - 1), :] = wzi
        f[xp(i - 1), :] = f[xp(i - 1), :] + rc[xp(i - 1), :] + fz + (up - low)
        return k1, h1, up

    k1, h1, low = lax.fori_loop(
        1, N, x_links, (k[xp(0), :], h[xp(0), :], jnp.zeros((N, L), jnp.float32)), unroll=4
    )
    wzi, fz = z_part(k1, h1)
    wz[xp(N - 1), :] = wzi
    f[xp(N - 1), :] = f[xp(N - 1), :] + rc[xp(N - 1), :] + fz - low

    for g in range(8):
        wzt[pl.ds(g, L, stride=8), :] = jnp.transpose(wz[pl.ds(g * L, L), :])

    one = jnp.ones((N, L), jnp.float32)

    def step(i, state, w, b_out, e_out, i_out):
        beta, ground, a = state
        e = w[xp(i + 1), :]
        inv = 1.0 / (beta + e + ground)
        bh = beta * inv
        eh = e * inv
        b_out[xp(i), :] = bh
        e_out[xp(i), :] = eh
        i_out[xp(i), :] = inv
        return bh * e, 1.0 + eh * ground, a + bh * ground

    def zrow(z):
        return pl.ds(pl.multiple_of(z * 8, 8), 8)

    def z_step(i, state):
        lo, hi = state
        e = wzt[zrow(i), :]
        inv = 1.0 / (lo + e)
        eh = e * inv
        ez[zrow(i), :] = eh
        iz[zrow(i), :] = inv
        lo = 1.0 + eh * lo
        t = L - 1 - i
        e = wzt[zrow(t - 1), :]
        inv = 1.0 / (hi + e)
        eh = e * inv
        ez[zrow(t), :] = eh
        iz[zrow(t), :] = inv
        hi = 1.0 + eh * hi
        return lo, hi

    def chains(i, state):
        sx, sy, sz = state
        sx = step(i, sx, wx, bx, ex, ix)
        sy = step(i, sy, wy, by, ey, iy)
        sz = z_step(2 * i - 2, sz)
        sz = z_step(2 * i - 1, sz)
        return sx, sy, sz

    zone = jnp.ones((8, L), jnp.float32)
    sx, sy, sz = lax.fori_loop(
        1,
        N - 1,
        chains,
        ((wx[xp(1), :], one, one), (wy[xp(1), :], one, one), (zone, zone)),
    )
    mx[0], mx[2], mx[1] = sx
    my[0], my[2], my[1] = sy
    for i in range(2 * N - 4, 2 * N - 1):
        sz = z_step(i, sz)
    lo, hi = sz
    mid = L // 2 - 1
    e = wzt[zrow(mid), :]
    inv = 1.0 / (hi + e)
    eh = e * inv
    ez[zrow(mid + 1), :] = eh
    iz[zrow(mid + 1), :] = inv
    iz[zrow(mid), :] = 1.0 / (lo + eh * hi)
    ez[zrow(mid), :] = jnp.zeros((8, L), jnp.float32)


def end_cell(w0, m):
    beta, a, ground = m[0], m[1], m[2]
    inv = 1.0 / (w0 + beta + a)
    wh = w0 * inv
    bh = beta * inv
    return (wh, bh, inv), (w0 * bh, wh * a, ground + bh * a)


def x_down_kernel(f_in, bx, ex, ix, mx, my, xlo, xhi, ylo, yhi, pxlo, pxhi, pylo, pyhi, out, s_out, cx, yout, f):
    south = link(COEF_Y, pylo[1], ylo[1])
    north = link(COEF_Y, yhi[1], pyhi[1])
    f[...] = f_in[...]
    f[yp(0), :] = f[yp(0), :] - 2.0 * south * (ylo[0] - pylo[0])
    f[yp(N - 1), :] = f[yp(N - 1), :] + 2.0 * north * (pyhi[0] - yhi[0])
    west = link(COEF_X, pxlo[1], xlo[1])
    east = link(COEF_X, xhi[1], pxhi[1])

    (wh, bh, inv), (mb, ma, mg) = end_cell(south, my)
    yout[0], yout[1], yout[2], yout[3], yout[4], yout[5] = wh, bh, inv, mb, ma, mg

    def step(i, state):
        s, r = state
        s_out[xp(i), :] = s * ix[xp(i), :]
        return f[xp(i + 1), :] + ex[xp(i), :] * s, r + bx[xp(i), :] * s

    s, r = lax.fori_loop(
        1, N - 1, step, (f[xp(1), :], jnp.zeros((N, L), jnp.float32)), unroll=5
    )
    s = s + 2.0 * east * (pxhi[0] - xhi[0])
    s0 = r + f[xp(0), :] - 2.0 * west * (xlo[0] - pxlo[0])
    (wh, bh, inv), (mb, ma, mg) = end_cell(west, mx)
    cx[0], cx[1], cx[2] = wh, bh, s0 * inv
    out[0], out[1], out[2], out[3], out[4] = mb, ma, mg, wh * s0, s + bh * s0


def ends_kernel(chunk, net, out):
    row = lax.broadcasted_iota(jnp.int32, (N, L), 0)

    def before(v, s):
        return jnp.where(row >= s, pltpu.roll(v, s, 0), 0.0)

    def after(v, s):
        return jnp.where(row < N - s, pltpu.roll(v, N - s, 0), 0.0)

    beta = net[0]
    ground = net[2] + after(net[1], chunk)
    rhs = net[4] + after(net[3], chunk)
    s = chunk
    while s < N:
        nxt = after(beta, s)
        inv = 1.0 / (ground + beta + nxt)
        gh, rh, bh = ground * inv, rhs * inv, beta * inv
        ground = ground + beta * before(gh, s) + nxt * after(gh, s)
        rhs = rhs + beta * before(rh, s) + nxt * after(rh, s)
        beta = beta * before(bh, s)
        s *= 2
    q = rhs / ground
    out[0] = before(q, chunk)
    out[1] = q


def x_up_kernel(ends, s_in, bx, ex, cx, by, ey, iy, ym, out, s_out, cy, d):
    last = ends[1]
    first = cx[2] + cx[0] * ends[0] + cx[1] * last
    d[xp(N - 1), :] = last
    d[xp(0), :] = first

    def back(t, nxt):
        i = N - 1 - t
        cur = (s_in[xp(i), :] + bx[xp(i), :] * first) + ex[xp(i), :] * nxt
        d[xp(i), :] = cur
        return cur

    lax.fori_loop(1, N - 1, back, last, unroll=5)

    def step(i, state):
        s, r = state
        s_out[xp(i), :] = s * iy[xp(i), :]
        return d[yp(i + 1), :] + ey[xp(i), :] * s, r + by[xp(i), :] * s

    s, r = lax.fori_loop(
        1, N - 1, step, (d[yp(1), :], jnp.zeros((N, L), jnp.float32)), unroll=5
    )
    s0 = r + d[yp(0), :]
    wh, bh, inv = ym[0], ym[1], ym[2]
    cy[...] = s0 * inv
    out[0], out[1], out[2], out[3], out[4] = ym[3], ym[4], ym[5], wh * s0, s + bh * s0


def final_kernel(ends, s_in, by, ey, ym, cy, ez, iz, h, out, d, t):
    last = ends[1]
    first = cy[...] + ym[0] * ends[0] + ym[1] * last
    d[yp(N - 1), :] = last
    d[yp(0), :] = first

    def back(u, nxt):
        j = N - 1 - u
        cur = (s_in[xp(j), :] + by[xp(j), :] * first) + ey[xp(j), :] * nxt
        d[yp(j), :] = cur
        return cur

    lax.fori_loop(1, N - 1, back, last, unroll=5)

    for g in range(8):
        t[pl.ds(g, L, stride=8), :] = jnp.transpose(d[pl.ds(g * L, L), :])

    def zrow(z):
        return pl.ds(pl.multiple_of(z * 8, 8), 8)

    mid = L // 2 - 1

    def down(i, state):
        lo, hi = state
        u = L - 1 - i
        t[zrow(i), :] = lo * iz[zrow(i), :]
        t[zrow(u), :] = hi * iz[zrow(u), :]
        return t[zrow(i + 1), :] + ez[zrow(i), :] * lo, t[zrow(u - 1), :] + ez[zrow(u), :] * hi

    lo, hi = lax.fori_loop(0, mid, down, (t[zrow(0), :], t[zrow(L - 1), :]), unroll=9)
    t[zrow(mid + 1), :] = hi * iz[zrow(mid + 1), :]
    m = (lo + ez[zrow(mid + 1), :] * hi) * iz[zrow(mid), :]
    t[zrow(mid), :] = m
    hi = t[zrow(mid + 1), :] + ez[zrow(mid + 1), :] * m
    t[zrow(mid + 1), :] = hi

    def up(i, state):
        lo, hi = state
        a = mid - i
        b = mid + 1 + i
        lo = t[zrow(a), :] + ez[zrow(a), :] * lo
        hi = t[zrow(b), :] + ez[zrow(b), :] * hi
        t[zrow(a), :] = lo
        t[zrow(b), :] = hi
        return lo, hi

    lax.fori_loop(1, mid + 1, up, (m, hi), unroll=9)
    for g in range(8):
        at = pl.ds(g * L, L)
        out[at, :] = h[at, :] + jnp.transpose(t[pl.ds(g, L, stride=8), :])


BLOCK = jax.ShapeDtypeStruct((ROWS, L), jnp.float32)


def planes(*lead):
    return jax.ShapeDtypeStruct(lead + (N, L), jnp.float32)


def call(kernel, outs, *args, scratch=(), flops=1000000):
    vmem = pl.BlockSpec(memory_space=pltpu.VMEM)
    moved = 4 * sum(a.size for a in args)
    return pl.pallas_call(
        kernel,
        out_shape=outs,
        in_specs=[vmem] * len(args),
        out_specs=jax.tree.map(lambda _: vmem, outs),
        scratch_shapes=[pltpu.VMEM(s.shape, s.dtype) for s in scratch],
        cost_estimate=pl.CostEstimate(flops=flops, bytes_accessed=moved, transcendentals=0),
    )(*args)


def neighbours(lo, hi, axis):
    count = lax.axis_size(axis)
    forward = [(i, i + 1) for i in range(count - 1)]
    backward = [(i + 1, i) for i in range(count - 1)]
    return lax.ppermute(hi, axis, forward), lax.ppermute(lo, axis, backward)


def line_ends(net, axis):
    count = lax.axis_size(axis)
    chunk = N // count
    got = lax.all_to_all(net, axis, 1, 1, tiled=True)
    ends = call(functools.partial(ends_kernel, chunk), planes(2), got, flops=100000)
    return lax.all_to_all(ends, axis, 1, 1, tiled=True)


def per_device(water_head, conductivity, recharge):
    h, k, rc = (a.reshape(ROWS, L) for a in (water_head, conductivity, recharge))
    xlo, xhi, ylo, yhi = call(pack_kernel, [planes(2)] * 4, h, k, flops=10000)
    pylo, pyhi = neighbours(ylo, yhi, "gy")
    pxlo, pxhi = neighbours(xlo, xhi, "gx")
    f, bx, ex, ix, mx, by, ey, iy, my, ez, iz = call(
        factor_kernel,
        [BLOCK] * 4 + [planes(3)] + [BLOCK] * 3 + [planes(3)] + [BLOCK] * 2,
        h,
        k,
        rc,
        scratch=[BLOCK] * 4,
        flops=20000000,
    )
    net, sx, cx, ym = call(
        x_down_kernel,
        [planes(5), BLOCK, planes(3), planes(6)],
        f, bx, ex, ix, mx, my, xlo, xhi, ylo, yhi, pxlo, pxhi, pylo, pyhi,
        scratch=[BLOCK],
    )
    ends = line_ends(net, "gx")
    net, sy, cy = call(
        x_up_kernel,
        [planes(5), BLOCK, planes()],
        ends, sx, bx, ex, cx, by, ey, iy, ym,
        scratch=[BLOCK],
    )
    ends = line_ends(net, "gy")
    out = call(
        final_kernel, BLOCK, ends, sy, by, ey, ym, cy, ez, iz, h, scratch=[BLOCK] * 2
    )
    return out.reshape(water_head.shape)


def solution(mesh):
    placed = (P("gx", "gy", None),) * 3
    return jax.shard_map(
        per_device, mesh=mesh, in_specs=placed, out_specs=P("gx", "gy", None), check_vma=False
    )
```

profile of v0, /device:TPU:1, one launch (start us, length us, event | category | flops | bytes accessed | tf_op | source)
XLA Modules:
  0.0 106.6 jit_solution(9084932252629445207)
XLA Ops:
  0.0 1.9 %shard_map.38 = (f32[2,32,128]{2,1,0:T(8,128)}, f32[2,32,128]{2,1,0:T(8,128)}, f32[2,32,128]{2,1,0:T(8,128)}, f32[2,32,128]{2,1,0:T(8,128)}) custom-call(f32[1024,128]{1,0:T(8,128)} %bitcast.4, f32[1024,128]{1,0:T(8,128)} %bitcast.7), custom_call_target="tpu_custom_call" | custom-call | flops 10000 | bytes 1048576 | tf_op jit(solution)/shard_map/pallas_call | solution.py:296
  1.9 1.3 %collective-permute-start.1 = (f32[2,32,128]{2,1,0:T(8,128)}, f32[2,32,128]{2,1,0:T(8,128)S(1)}, u32[]{:S(2)}, u32[]{:S(2)}) collective-permute-start(f32[2,32,128]{2,1,0:T(8,128)} %get-tuple-element.33.xlo), channel_id=1, source_target_pairs={{16,0},{32,16},{48,32},{64,48},{80,64},{96,80},{112,96},{128,112},... | collective-permute-start | bytes 98312 | tf_op jit(solution)/shard_map/ppermute | solution.py:310
  3.1 4.6 %collective-permute-start = (f32[2,32,128]{2,1,0:T(8,128)}, f32[2,32,128]{2,1,0:T(8,128)S(1)}, u32[]{:S(2)}, u32[]{:S(2)}) collective-permute-start(f32[2,32,128]{2,1,0:T(8,128)} %get-tuple-element.34.xhi), channel_id=1, source_target_pairs={{0,16},{16,32},{32,48},{48,64},{64,80},{80,96},{96,112},{112,128},... | collective-permute-start | bytes 98312 | tf_op jit(solution)/shard_map/ppermute | solution.py:310
  7.7 8.7 %collective-permute-start.3 = (f32[2,32,128]{2,1,0:T(8,128)}, f32[2,32,128]{2,1,0:T(8,128)S(1)}, u32[]{:S(2)}, u32[]{:S(2)}) collective-permute-start(f32[2,32,128]{2,1,0:T(8,128)} %get-tuple-element.35.ylo), channel_id=1, source_target_pairs={{1,0},{2,1},{3,2},{4,3},{5,4},{6,5},{7,6},{8,7},{9,8},{10,9},{11,1... | collective-permute-start | bytes 98312 | tf_op jit(solution)/shard_map/ppermute | solution.py:310
  16.5 1.9 %collective-permute-start.2 = (f32[2,32,128]{2,1,0:T(8,128)}, f32[2,32,128]{2,1,0:T(8,128)S(1)}, u32[]{:S(2)}, u32[]{:S(2)}) collective-permute-start(f32[2,32,128]{2,1,0:T(8,128)} %get-tuple-element.36.yhi), channel_id=1, source_target_pairs={{0,1},{1,2},{2,3},{3,4},{4,5},{5,6},{6,7},{7,8},{8,9},{9,10},{10,1... | collective-permute-start | bytes 98312 | tf_op jit(solution)/shard_map/ppermute | solution.py:310
  18.4 7.5 %shard_map.37 = (f32[1024,128]{1,0:T(8,128)}, f32[1024,128]{1,0:T(8,128)}, f32[1024,128]{1,0:T(8,128)}, f32[1024,128]{1,0:T(8,128)}, f32[3,32,128]{2,1,0:T(8,128...) custom-call(f32[1024,128]{1,0:T(8,128)} %bitcast.5, ...), custom_call_target="tpu_custom_call" | custom-call | flops 20000000 | bytes 1572864 | tf_op jit(solution)/shard_map/pallas_call | solution.py:296
  25.9 0.0 collective-permute-done.1.pxhi
  25.9 0.0 collective-permute-done.pxlo
  25.9 0.0 collective-permute-done.3.pyhi
  25.9 0.0 copy-start.2
  25.9 0.0 collective-permute-done.2.pylo
  26.0 0.5 copy-done
  26.5 0.0 copy-done.1
  26.5 0.0 copy-done.2
  26.5 0.0 copy-done.3
  26.6 2.7 %shard_map.39 = (f32[5,32,128]{2,1,0:T(8,128)}, f32[1024,128]{1,0:T(8,128)}, f32[3,32,128]{2,1,0:T(8,128)}, f32[6,32,128]{2,1,0:T(8,128)}) custom-call(f32[1024,128]{1,0:T(8,128)} %get-tuple-element.27.f_in, f32[1024,128]{1,0:T(8,128)} %get-tuple-element.28.bx, f32[1024,128]{1,0:T(8,128)} %get-tuple-element.29.ex, f32[1024,128]{1,0:T(8,128)} %get-tuple-element.30.ix, ...), custom_call_target="tpu_custom_call" | custom-call | flops 1000000 | bytes 2457600 | tf_op jit(solution)/shard_map/pallas_call | solution.py:296
  29.3 0.9 copy.4
  30.2 17.9 %all_to_all.20 = f32[5,32,128]{2,0,1:T(8,128)S(1)} all-to-all(f32[5,32,128]{2,0,1:T(8,128)S(1)} %copy.4), channel_id=1, replica_groups=mesh['gx'=32,'gy'=16] {'gx'}, dimensions={1} | all-to-all | bytes 163840 | tf_op jit(solution)/shard_map/all_to_all | solution.py:316
  48.1 0.7 copy.5.net
  48.8 1.6 %shard_map.40 = f32[2,32,128]{2,1,0:T(8,128)} custom-call(f32[5,32,128]{2,1,0:T(8,128)} %copy.5.net), custom_call_target="tpu_custom_call" | custom-call | flops 100000 | bytes 81920 | tf_op jit(solution)/shard_map/pallas_call | solution.py:296
  50.4 0.8 copy.6
  51.1 11.8 %all_to_all.21 = f32[2,32,128]{2,0,1:T(2,128)S(1)} all-to-all(f32[2,32,128]{2,0,1:T(2,128)S(1)} %copy.6), channel_id=1, replica_groups=mesh['gx'=32,'gy'=16] {'gx'}, dimensions={1} | all-to-all | bytes 65536 | tf_op jit(solution)/shard_map/all_to_all | solution.py:318
  63.0 0.6 copy.7.ends
  63.6 3.2 %shard_map.41 = (f32[5,32,128]{2,1,0:T(8,128)}, f32[1024,128]{1,0:T(8,128)}, f32[32,128]{1,0:T(8,128)}) custom-call(f32[2,32,128]{2,1,0:T(8,128)} %copy.7.ends, f32[1024,128]{1,0:T(8,128)} %get-tuple-element.38.s_in, f32[1024,128]{1,0:T(8,128)} %get-tuple-element.28.bx, f32[1024,128]{1,0:T(8,128)} %get-tuple-element.29.ex, ...), custom_call_target="tpu_custom_call" | custom-call | flops 1000000 | bytes 3325952 | tf_op jit(solution)/shard_map/pallas_call | solution.py:296
  66.8 0.9 copy.8
  67.7 20.9 %all_to_all.22 = f32[5,32,128]{2,0,1:T(8,128)S(1)} all-to-all(f32[5,32,128]{2,0,1:T(8,128)S(1)} %copy.8), channel_id=1, replica_groups=mesh['gx'=32,'gy'=16] {'gy'}, dimensions={1} | all-to-all | bytes 163840 | tf_op jit(solution)/shard_map/all_to_all | solution.py:316
  88.7 0.7 copy.9.net
  89.3 1.6 %shard_map.42 = f32[2,32,128]{2,1,0:T(8,128)} custom-call(f32[5,32,128]{2,1,0:T(8,128)} %copy.9.net), custom_call_target="tpu_custom_call" | custom-call | flops 100000 | bytes 81920 | tf_op jit(solution)/shard_map/pallas_call | solution.py:296
  90.9 0.8 copy.10
  91.7 10.1 %all_to_all.23 = f32[2,32,128]{2,0,1:T(2,128)S(1)} all-to-all(f32[2,32,128]{2,0,1:T(2,128)S(1)} %copy.10), channel_id=1, replica_groups=mesh['gx'=32,'gy'=16] {'gy'}, dimensions={1} | all-to-all | bytes 65536 | tf_op jit(solution)/shard_map/all_to_all | solution.py:318
  101.8 0.6 copy.11.ends
  102.4 4.2 %shard_map.43 = f32[1024,128]{1,0:T(8,128)} custom-call(f32[2,32,128]{2,1,0:T(8,128)} %copy.11.ends, f32[1024,128]{1,0:T(8,128)} %get-tuple-element.45.s_in, f32[1024,128]{1,0:T(8,128)} %get-tuple-element.40.by, f32[1024,128]{1,0:T(8,128)} %get-tuple-element.41.ey, f32[6,32,128]{2,1,0:T(8,128)} %get-tuple-element.43.ym, f32[32,128]{1,0:T(8,128)} %get-tuple-element.46.cy, ...), custom_call_target="tpu_custom_call" | custom-call | flops 1000000 | bytes 3293184 | tf_op jit(solution)/shard_map/pallas_call | solution.py:296
  (3 shorter events, 0.0 us)
Async XLA Ops:
  1.9 24.0 %collective-permute-start.1 = (f32[2,32,128]{2,1,0:T(8,128)}, f32[2,32,128]{2,1,0:T(8,128)S(1)}, u32[]{:S(2)}, u32[]{:S(2)}) collective-permute-start(f32[2,32,128]{2,1,0:T(8,128)} %get-tuple-element.33.xlo), channel_id=1, source_target_pairs={{16,0},{32,16},{48,32},{64,48},{80,64},{96,80},{112,96},{128,112},... | collective-permute-start | bytes 98312 | tf_op jit(solution)/shard_map/ppermute | solution.py:310
  3.1 22.8 %collective-permute-start = (f32[2,32,128]{2,1,0:T(8,128)}, f32[2,32,128]{2,1,0:T(8,128)S(1)}, u32[]{:S(2)}, u32[]{:S(2)}) collective-permute-start(f32[2,32,128]{2,1,0:T(8,128)} %get-tuple-element.34.xhi), channel_id=1, source_target_pairs={{0,16},{16,32},{32,48},{48,64},{64,80},{80,96},{96,112},{112,128},... | collective-permute-start | bytes 98312 | tf_op jit(solution)/shard_map/ppermute | solution.py:310
  7.7 18.2 %collective-permute-start.3 = (f32[2,32,128]{2,1,0:T(8,128)}, f32[2,32,128]{2,1,0:T(8,128)S(1)}, u32[]{:S(2)}, u32[]{:S(2)}) collective-permute-start(f32[2,32,128]{2,1,0:T(8,128)} %get-tuple-element.35.ylo), channel_id=1, source_target_pairs={{1,0},{2,1},{3,2},{4,3},{5,4},{6,5},{7,6},{8,7},{9,8},{10,9},{11,1... | collective-permute-start | bytes 98312 | tf_op jit(solution)/shard_map/ppermute | solution.py:310
  16.5 9.5 %collective-permute-start.2 = (f32[2,32,128]{2,1,0:T(8,128)}, f32[2,32,128]{2,1,0:T(8,128)S(1)}, u32[]{:S(2)}, u32[]{:S(2)}) collective-permute-start(f32[2,32,128]{2,1,0:T(8,128)} %get-tuple-element.36.yhi), channel_id=1, source_target_pairs={{0,1},{1,2},{2,3},{3,4},{4,5},{5,6},{6,7},{7,8},{8,9},{9,10},{10,1... | collective-permute-start | bytes 98312 | tf_op jit(solution)/shard_map/ppermute | solution.py:310
  25.9 0.6 copy-start
  25.9 0.6 copy-start.1
  25.9 0.6 copy-start.2
  26.0 0.6 copy-start.3
where the time goes:
time: 107 us
  blocking collectives  60.7 us (57%)
  Pallas kernels  22.7 us (21%)
  starting transfers between devices  16.5 us (15%)
  local copies, waits for them, and re-layouts  6.56 us (6%)
    all_to_all x2, blocking collectives, line_ends(): got = lax.all_to_all(net, axis, 1, 1, tiled=True)  38.8 us
    pallas_call x7, Pallas kernels, call(): pl.pallas_call(kernel, out_shape=outs, in_specs=[vmem] * len(args), out_s...  22.7 us
    all_to_all x2, blocking collectives, line_ends(): return lax.all_to_all(ends, axis, 1, 1, tiled=True)  21.9 us
    ppermute x4, starting transfers between devices, neighbours(): return (lax.ppermute(hi, axis, forward), lax.ppermute(lo, axis, backward))  16.5 us
    pallas_call x4, local copies, waits for them, and re-layouts, call(): pl.pallas_call(kernel, out_shape=outs, in_specs=[vmem] * len(args), out_s...  3.45 us
  transfers between devices with their start and end apart: 4, of which 0 were waited for; matrix products, arithmetic and copies ran while one was open for 0% of the time, Pallas kernels for 7%

commit v1 on v0

v1 whole, which is shorter than its diff:
```python
import functools

import jax
import jax.numpy as jnp
from jax import lax
from jax.experimental import pallas as pl
from jax.experimental.pallas import tpu as pltpu
from jax.sharding import PartitionSpec as P

COEF_Z = 8.0
COEF_X = 5120.0
COEF_Y = 5120.0

N = 32
L = 128
ROWS = N * N
ROW = 8
VMEM_LIMIT = 24 << 20


def link(coef, one, other):
    return coef * (one * other) / (one + other)


def xp(i):
    return pl.ds(pl.multiple_of(i * N, N), N)


def yp(j):
    return pl.ds(j, N, stride=N)


def zp(z):
    return pl.ds(pl.multiple_of(z * 8, 8), 8)


def pack_kernel(h, k, ylo, yhi):
    for out, at in ((ylo, yp(0)), (yhi, yp(N - 1))):
        out[0] = h[at, :]
        out[1] = k[at, :]


def factor_kernel(h, k, rc, f, bx, ex, ix, mx, by, ey, iy, my, ez, iz, wx, wy, wz, wzt):
    def y_links(j, carry):
        k0, h0, low = carry
        k1, h1 = k[yp(j), :], h[yp(j), :]
        w = link(COEF_Y, k0, k1)
        wy[xp(j), :] = w
        up = 2.0 * w * (h1 - h0)
        f[yp(j - 1), :] = up - low
        return k1, h1, up

    _, _, low = lax.fori_loop(
        1, N, y_links, (k[yp(0), :], h[yp(0), :], jnp.zeros((N, L), jnp.float32)), unroll=4
    )
    f[yp(N - 1), :] = -low

    lane = lax.broadcasted_iota(jnp.int32, (N, L), 1)

    def planes_x(i, k0):
        h0 = h[xp(i), :]
        ku = pltpu.roll(k0, L - 1, 1)
        hu = pltpu.roll(h0, L - 1, 1)
        w = jnp.where(lane < L - 1, link(COEF_Z, k0, ku), 0.0)
        wz[xp(i), :] = w
        up = 2.0 * w * (hu - h0)
        f[xp(i), :] = f[xp(i), :] + rc[xp(i), :] + 2.0 * h0 + (up - pltpu.roll(up, 1, 1))
        k1 = k[xp(jnp.minimum(i + 1, N - 1)), :]
        wx[xp(i), :] = link(COEF_X, k0, k1)
        return k1

    lax.fori_loop(0, N, planes_x, k[xp(0), :], unroll=4)

    for g in range(8):
        wzt[pl.ds(g, L, stride=8), :] = jnp.transpose(wz[pl.ds(g * L, L), :])

    one = jnp.ones((N, L), jnp.float32)

    def step(i, state, e, b_out, e_out, i_out):
        beta, ground, a = state
        inv = 1.0 / (beta + e + ground)
        bh = beta * inv
        eh = e * inv
        b_out[xp(i), :] = bh
        e_out[xp(i), :] = eh
        i_out[xp(i), :] = inv
        return bh * e, 1.0 + eh * ground, a + bh * ground

    def z_step(i, state):
        lo, hi = state
        e = wzt[zp(i), :]
        inv = 1.0 / (lo + e)
        eh = e * inv
        ez[zp(i), :] = eh
        iz[zp(i), :] = inv
        lo = 1.0 + eh * lo
        t = L - 1 - i
        e = wzt[zp(t - 1), :]
        inv = 1.0 / (hi + e)
        eh = e * inv
        ez[zp(t), :] = eh
        iz[zp(t), :] = inv
        hi = 1.0 + eh * hi
        return lo, hi

    def chains(i, state):
        sx, sy, sz = state
        sx = step(i, sx, wx[xp(i), :], bx, ex, ix)
        sy = step(i, sy, wy[xp(i + 1), :], by, ey, iy)
        sz = z_step(2 * i - 2, sz)
        sz = z_step(2 * i - 1, sz)
        return sx, sy, sz

    zone = jnp.ones((8, L), jnp.float32)
    sx, sy, sz = lax.fori_loop(
        1,
        N - 1,
        chains,
        ((wx[xp(0), :], one, one), (wy[xp(1), :], one, one), (zone, zone)),
    )
    mx[0], mx[2], mx[1] = sx
    my[0], my[2], my[1] = sy
    for i in range(2 * N - 4, 2 * N - 1):
        sz = z_step(i, sz)
    lo, hi = sz
    mid = L // 2 - 1
    e = wzt[zp(mid), :]
    inv = 1.0 / (hi + e)
    eh = e * inv
    ez[zp(mid + 1), :] = eh
    iz[zp(mid + 1), :] = inv
    iz[zp(mid), :] = 1.0 / (lo + eh * hi)
    ez[zp(mid), :] = jnp.zeros((8, L), jnp.float32)


def send_segment(out, m, s0, s1, k0, k1):
    for at, value in enumerate((m[0], m[1], m[2], s0, s1, k0, k1)):
        out[pl.ds(at, N, stride=ROW), :] = value


def x_down_kernel(f_in, bx, ex, ix, mx, k, ylo, yhi, pylo, pyhi, out, s_out, f):
    south = link(COEF_Y, pylo[1], ylo[1])
    north = link(COEF_Y, yhi[1], pyhi[1])
    f[...] = f_in[...]
    f[yp(0), :] = f[yp(0), :] - 2.0 * south * (ylo[0] - pylo[0])
    f[yp(N - 1), :] = f[yp(N - 1), :] + 2.0 * north * (pyhi[0] - yhi[0])

    def step(i, state):
        s, r = state
        s_out[xp(i), :] = s * ix[xp(i), :]
        return f[xp(i + 1), :] + ex[xp(i), :] * s, r + bx[xp(i), :] * s

    s, r = lax.fori_loop(1, N - 1, step, (f[xp(1), :], f[xp(0), :]), unroll=5)
    send_segment(out, mx, r, s, k[xp(0), :], k[xp(N - 1), :])


def ends_kernel(chunk, coef, net, out):
    row = lax.broadcasted_iota(jnp.int32, (N, L), 0)

    def before(v, s):
        return jnp.where(row >= s, pltpu.roll(v, s, 0), 0.0)

    def after(v, s):
        return jnp.where(row < N - s, pltpu.roll(v, N - s, 0), 0.0)

    inner, c0, c1, s0, s1, k0, k1 = (net[pl.ds(at, N, stride=ROW), :] for at in range(7))
    w = link(coef, before(k1, chunk), k0)
    inv0 = 1.0 / (w + inner + c0)
    wh, bh = w * inv0, inner * inv0
    beta = w * bh
    ground = c1 + bh * c0 + after(wh * c0, chunk)
    rhs = s1 + bh * s0 + after(wh * s0, chunk)
    s = chunk
    while s < N:
        nxt = after(beta, s)
        inv = 1.0 / (ground + beta + nxt)
        gh, rh, lh = ground * inv, rhs * inv, beta * inv
        ground = ground + beta * before(gh, s) + nxt * after(gh, s)
        rhs = rhs + beta * before(rh, s) + nxt * after(rh, s)
        beta = beta * before(lh, s)
        s *= 2
    q = rhs / ground
    out[pl.ds(0, N, stride=2), :] = s0 * inv0 + wh * before(q, chunk) + bh * q
    out[pl.ds(1, N, stride=2), :] = q


def x_up_kernel(ends, s_in, bx, ex, h, by, ey, iy, my, ylo, yhi, out, s_out, d):
    first = ends[pl.ds(0, N, stride=2), :]
    last = ends[pl.ds(1, N, stride=2), :]
    d[xp(N - 1), :] = last - 2.0 * h[xp(N - 1), :]
    d[xp(0), :] = first - 2.0 * h[xp(0), :]

    def back(t, nxt):
        i = N - 1 - t
        cur = (s_in[xp(i), :] + bx[xp(i), :] * first) + ex[xp(i), :] * nxt
        d[xp(i), :] = cur - 2.0 * h[xp(i), :]
        return cur

    lax.fori_loop(1, N - 1, back, last, unroll=5)

    def step(i, state):
        s, r = state
        s_out[xp(i), :] = s * iy[xp(i), :]
        return d[yp(i + 1), :] + ey[xp(i), :] * s, r + by[xp(i), :] * s

    s, r = lax.fori_loop(1, N - 1, step, (d[yp(1), :], d[yp(0), :]), unroll=5)
    send_segment(out, my, r, s, ylo[1], yhi[1])


def final_kernel(ends, s_in, by, ey, ez, iz, h, out, d, t):
    first = ends[pl.ds(0, N, stride=2), :]
    last = ends[pl.ds(1, N, stride=2), :]
    d[yp(N - 1), :] = last
    d[yp(0), :] = first

    def back(u, nxt):
        j = N - 1 - u
        cur = (s_in[xp(j), :] + by[xp(j), :] * first) + ey[xp(j), :] * nxt
        d[yp(j), :] = cur
        return cur

    lax.fori_loop(1, N - 1, back, last, unroll=5)

    for g in range(8):
        t[pl.ds(g, L, stride=8), :] = jnp.transpose(d[pl.ds(g * L, L), :])

    mid = L // 2 - 1

    def down(i, state):
        lo, hi = state
        u = L - 1 - i
        t[zp(i), :] = lo * iz[zp(i), :]
        t[zp(u), :] = hi * iz[zp(u), :]
        return t[zp(i + 1), :] + ez[zp(i), :] * lo, t[zp(u - 1), :] + ez[zp(u), :] * hi

    lo, hi = lax.fori_loop(0, mid, down, (t[zp(0), :], t[zp(L - 1), :]), unroll=9)
    t[zp(mid + 1), :] = hi * iz[zp(mid + 1), :]
    m = (lo + ez[zp(mid + 1), :] * hi) * iz[zp(mid), :]
    t[zp(mid), :] = m
    hi = t[zp(mid + 1), :] + ez[zp(mid + 1), :] * m
    t[zp(mid + 1), :] = hi

    def up(i, state):
        lo, hi = state
        a = mid - i
        b = mid + 1 + i
        lo = t[zp(a), :] + ez[zp(a), :] * lo
        hi = t[zp(b), :] + ez[zp(b), :] * hi
        t[zp(a), :] = lo
        t[zp(b), :] = hi
        return lo, hi

    lax.fori_loop(1, mid + 1, up, (m, hi), unroll=9)
    for g in range(8):
        at = pl.ds(g * L, L)
        out[at, :] = h[at, :] + jnp.transpose(t[pl.ds(g, L, stride=8), :])


BLOCK = (ROWS, L)
NET = (N * ROW, L)
ENDS = (N * 2, L)


def planes(*lead):
    return lead + (N, L)


def call(kernel, outs, *args, scratch=(), in_vmem=(), out_vmem=True, flops=1000000):
    vmem = pl.BlockSpec(memory_space=pltpu.VMEM)
    moved = 4 * sum(a.size for a in args)
    args = [pltpu.with_memory_space_constraint(a, pltpu.VMEM) if i in in_vmem else a for i, a in enumerate(args)]
    make = pltpu.VMEM if out_vmem else jax.ShapeDtypeStruct
    return pl.pallas_call(
        kernel,
        out_shape=[make(s, jnp.float32) for s in outs],
        in_specs=[vmem] * len(args),
        out_specs=[vmem] * len(outs),
        scratch_shapes=[pltpu.VMEM(s, jnp.float32) for s in scratch],
        compiler_params=pltpu.CompilerParams(vmem_limit_bytes=VMEM_LIMIT),
        cost_estimate=pl.CostEstimate(flops=flops, bytes_accessed=moved, transcendentals=0),
    )(*args)


def neighbours(lo, hi, axis):
    count = lax.axis_size(axis)
    forward = [(i, i + 1) for i in range(count - 1)]
    backward = [(i + 1, i) for i in range(count - 1)]
    return lax.ppermute(hi, axis, forward), lax.ppermute(lo, axis, backward)


def line_ends(net, axis, coef):
    chunk = N // lax.axis_size(axis)
    got = lax.all_to_all(net.reshape(N, ROW, L), axis, 0, 0, tiled=True).reshape(NET)
    (ends,) = call(functools.partial(ends_kernel, chunk, coef), [ENDS], got, in_vmem=(0,), flops=100000)
    return lax.all_to_all(ends.reshape(N, 2, L), axis, 0, 0, tiled=True).reshape(ENDS)


def per_device(water_head, conductivity, recharge):
    h, k, rc = (a.reshape(ROWS, L) for a in (water_head, conductivity, recharge))
    ylo, yhi = call(pack_kernel, [planes(2)] * 2, h, k, flops=10000)
    pylo, pyhi = neighbours(ylo, yhi, "gy")
    f, bx, ex, ix, mx, by, ey, iy, my, ez, iz = call(
        factor_kernel,
        [BLOCK] * 4 + [planes(3)] + [BLOCK] * 3 + [planes(3)] + [BLOCK] * 2,
        h,
        k,
        rc,
        scratch=[BLOCK] * 4,
        flops=20000000,
    )
    net, sx = call(
        x_down_kernel,
        [NET, BLOCK],
        f, bx, ex, ix, mx, k, ylo, yhi, pylo, pyhi,
        in_vmem=(0, 1, 2, 3, 4, 6, 7, 8, 9),
        scratch=[BLOCK],
    )
    ends = line_ends(net, "gx", COEF_X)
    net, sy = call(
        x_up_kernel,
        [NET, BLOCK],
        ends, sx, bx, ex, h, by, ey, iy, my, ylo, yhi,
        in_vmem=(0, 1, 2, 3, 5, 6, 7, 8, 9, 10),
        scratch=[BLOCK],
    )
    ends = line_ends(net, "gy", COEF_Y)
    (out,) = call(
        final_kernel,
        [BLOCK],
        ends, sy, by, ey, ez, iz, h,
        in_vmem=(0, 1, 2, 3, 4, 5),
        out_vmem=False,
        scratch=[BLOCK] * 2,
    )
    return out.reshape(water_head.shape)


def solution(mesh):
    placed = (P("gx", "gy", None),) * 3
    return jax.shard_map(
        per_device, mesh=mesh, in_specs=placed, out_specs=P("gx", "gy", None), check_vma=False
    )
```

time: 107 us -> 79.2 us (0.74)
  Pallas kernels: 22.7 us -> 6.95 us
  starting transfers between devices: 16.5 us -> 10.8 us
  local copies, waits for them, and re-layouts: 6.56 us -> 2.1 us
  blocking collectives: 60.7 us -> 58.8 us
    pallas_call x7, Pallas kernels: 22.7 us -> 6.95 us  [call(): pl.pallas_call(kernel, out_shape=[make(s, jnp.float32) for s in outs], in...]
    ppermute x4 -> x2, starting transfers between devices: 16.5 us -> 10.8 us  [neighbours(): return (lax.ppermute(hi, axis, forward), lax.ppermute(lo, axis, backward))]
    pallas_call x4 -> x0, local copies, waits for them, and re-layouts: 3.45 us -> none  [call(): pl.pallas_call(kernel, out_shape=outs, in_specs=[vmem] * len(args), out_s...]
    all_to_all x4 -> x0, local copies, waits for them, and re-layouts: 2.51 us -> none  [the longest x2 1.3 us: line_ends(): got = lax.all_to_all(net, axis, 1, 1, tiled=True)]
    all_to_all x4, blocking collectives: 60.7 us -> 58.8 us  [the longest x2 37 us: line_ends(): lax.all_to_all(net.reshape(N, ROW, L), axis, 0, 0, tiled=True).reshape(NET)]
    unnamed x8 -> x10, local copies, waits for them, and re-layouts: 0.6 us -> 2.1 us
  transfers between devices with their start and end apart: 4 -> 2, of which waited for: 0 -> 0; matrix products, arithmetic and copies ran while one was open for 0% -> 0% of each run, Pallas kernels for 7% -> 4%
where the time goes in v1:
time: 79.2 us; the launch traced here: 78.8 us
  blocking collectives  58.8 us (74%)
  starting transfers between devices  10.8 us (14%)
  Pallas kernels  6.95 us (9%)
  local copies, waits for them, and re-layouts  2.1 us (3%)
    all_to_all x2, blocking collectives, line_ends(): lax.all_to_all(net.reshape(N, ROW, L), axis, 0, 0, tiled=True).reshape(NET)  37 us
    all_to_all x2, blocking collectives, line_ends(): lax.all_to_all(ends.reshape(N, 2, L), axis, 0, 0, tiled=True).reshape(ENDS)  21.9 us
    ppermute x2, starting transfers between devices, neighbours(): return (lax.ppermute(hi, axis, forward), lax.ppermute(lo, axis, backward))  10.8 us
    pallas_call x7, Pallas kernels, call(): pl.pallas_call(kernel, out_shape=[make(s, jnp.float32) for s in outs], in...  6.95 us
    unnamed x10, local copies, waits for them, and re-layouts  2.1 us
  transfers between devices with their start and end apart: 2, of which 0 were waited for; matrix products, arithmetic and copies ran while one was open for 0% of the time, Pallas kernels for 4%

profile of v1, /device:TPU:1, one launch (start us, length us, event | category | flops | bytes accessed | tf_op | source)
XLA Modules:
  0.0 78.8 jit_solution(2574403344145969459)
XLA Ops:
  0.0 0.0 copy-start
  0.0 1.0 %copy-done = f32[32,32,128]{2,1,0:T(8,128)S(1)} copy-done((f32[32,32,128]{2,1,0:T(8,128)S(1)}, f32[32,32,128]{2,1,0:T(8,128)}, u32[]{:S(2)}) %copy-start) | copy-done | bytes 524312
  1.0 0.0 copy-start.2
  1.0 1.0 %copy-done.2 = f32[32,32,128]{2,1,0:T(8,128)S(1)} copy-done((f32[32,32,128]{2,1,0:T(8,128)S(1)}, f32[32,32,128]{2,1,0:T(8,128)}, u32[]{:S(2)}) %copy-start.2) | copy-done | bytes 524312
  2.1 0.0 copy-start.4
  2.1 0.1 shard_map.38
  2.1 8.9 %collective-permute-start.1 = (f32[2,32,128]{2,1,0:T(8,128)S(1)}, f32[2,32,128]{2,1,0:T(8,128)S(1)}, u32[]{:S(2)}, u32[]{:S(2)}) collective-permute-start(f32[2,32,128]{2,1,0:T(8,128)S(1)} %get-tuple-element.27.ylo), channel_id=1, source_target_pairs={{1,0},{2,1},{3,2},{4,3},{5,4},{6,5},{7,6},{8,7},{9,8},{10,9},{11,1... | collective-permute-start | bytes 98312 | tf_op jit(solution)/shard_map/ppermute | solution.py:288
  11.0 1.9 %collective-permute-start = (f32[2,32,128]{2,1,0:T(8,128)S(1)}, f32[2,32,128]{2,1,0:T(8,128)S(1)}, u32[]{:S(2)}, u32[]{:S(2)}) collective-permute-start(f32[2,32,128]{2,1,0:T(8,128)S(1)} %get-tuple-element.28.yhi), channel_id=1, source_target_pairs={{0,1},{1,2},{2,3},{3,4},{4,5},{5,6},{6,7},{7,8},{8,9},{9,10},{10,1... | collective-permute-start | bytes 98312 | tf_op jit(solution)/shard_map/ppermute | solution.py:288
  13.0 0.0 copy-done.4
  13.0 0.0 copy-start.3
  13.0 3.5 %shard_map.37 = (f32[1024,128]{1,0:T(8,128)S(1)}, f32[1024,128]{1,0:T(8,128)S(1)}, f32[1024,128]{1,0:T(8,128)S(1)}, f32[1024,128]{1,0:T(8,128)S(1)}, f32[3,32,12...) custom-call(f32[1024,128]{1,0:T(8,128)S(1)} %bitcast.13, ...), custom_call_target="tpu_custom_call" | custom-call | flops 20000000 | bytes 1572864 | tf_op jit(solution)/shard_map/pallas_call | solution.py:273
  16.5 0.0 collective-permute-done.1.pyhi
  16.5 0.0 collective-permute-done.pylo
  16.5 0.0 copy-done.3
  16.5 0.0 copy-start.1
  16.6 0.2 shard_map.39
  16.8 16.0 %all_to_all.20 = f32[32,8,128]{2,1,0:T(8,128)S(1)} all-to-all(f32[32,8,128]{2,1,0:T(8,128)S(1)} %bitcast.27), channel_id=1, replica_groups=mesh['gx'=32,'gy'=16] {'gx'}, dimensions={0} | all-to-all | bytes 262144 | tf_op jit(solution)/shard_map/all_to_all | solution.py:293
  32.8 0.1 shard_map.40
  32.9 11.8 %all_to_all.21 = f32[32,2,128]{2,1,0:T(2,128)S(1)} all-to-all(f32[32,2,128]{2,1,0:T(2,128)S(1)} %bitcast.24), channel_id=1, replica_groups=mesh['gx'=32,'gy'=16] {'gx'}, dimensions={0} | all-to-all | bytes 65536 | tf_op jit(solution)/shard_map/all_to_all | solution.py:295
  44.7 0.0 copy-done.1
  44.8 0.6 shard_map.41
  45.4 20.9 %all_to_all.22 = f32[32,8,128]{2,1,0:T(8,128)S(1)} all-to-all(f32[32,8,128]{2,1,0:T(8,128)S(1)} %bitcast.26), channel_id=1, replica_groups=mesh['gx'=32,'gy'=16] {'gy'}, dimensions={0} | all-to-all | bytes 262144 | tf_op jit(solution)/shard_map/all_to_all | solution.py:293
  66.3 0.1 shard_map.42
  66.4 10.1 %all_to_all.23 = f32[32,2,128]{2,1,0:T(2,128)S(1)} all-to-all(f32[32,2,128]{2,1,0:T(2,128)S(1)} %bitcast.25), channel_id=1, replica_groups=mesh['gx'=32,'gy'=16] {'gy'}, dimensions={0} | all-to-all | bytes 65536 | tf_op jit(solution)/shard_map/all_to_all | solution.py:295
  76.5 2.3 %shard_map.43 = f32[1024,128]{1,0:T(8,128)} custom-call(f32[64,128]{1,0:T(8,128)S(1)} %bitcast.23, f32[1024,128]{1,0:T(8,128)S(1)} %get-tuple-element.36.s_in, f32[1024,128]{1,0:T(8,128)S(1)} %get-tuple-element.31.by, f32[1024,128]{1,0:T(8,128)S(1)} %get-tuple-element.32.ey, f32[1024,128]{1,0:T(8,128)S(1)} %get-tuple-element.37.ez, ...), custom_call_target="tpu_custom_call" | custom-call | flops 1000000 | bytes 3178496 | tf_op jit(solution)/shard_map/pallas_call | solution.py:273
Async XLA Ops:
  0.0 1.0 %copy-start = (f32[32,32,128]{2,1,0:T(8,128)S(1)}, f32[32,32,128]{2,1,0:T(8,128)}, u32[]{:S(2)}) copy-start(f32[32,32,128]{2,1,0:T(8,128)} %param.3) | copy-start | bytes 1572868
  1.0 1.0 %copy-start.2 = (f32[32,32,128]{2,1,0:T(8,128)S(1)}, f32[32,32,128]{2,1,0:T(8,128)}, u32[]{:S(2)}) copy-start(f32[32,32,128]{2,1,0:T(8,128)} %param.4) | copy-start | bytes 1572868
  2.1 10.9 %copy-start.4 = (f32[32,32,128]{2,1,0:T(8,128)S(1)}, f32[32,32,128]{2,1,0:T(8,128)}, u32[]{:S(2)}) copy-start(f32[32,32,128]{2,1,0:T(8,128)} %param.5) | copy-start | bytes 1572868
  2.1 14.4 %collective-permute-start.1 = (f32[2,32,128]{2,1,0:T(8,128)S(1)}, f32[2,32,128]{2,1,0:T(8,128)S(1)}, u32[]{:S(2)}, u32[]{:S(2)}) collective-permute-start(f32[2,32,128]{2,1,0:T(8,128)S(1)} %get-tuple-element.27.ylo), channel_id=1, source_target_pairs={{1,0},{2,1},{3,2},{4,3},{5,4},{6,5},{7,6},{8,7},{9,8},{10,9},{11,1... | collective-permute-start | bytes 98312 | tf_op jit(solution)/shard_map/ppermute | solution.py:288
  11.0 5.5 %collective-permute-start = (f32[2,32,128]{2,1,0:T(8,128)S(1)}, f32[2,32,128]{2,1,0:T(8,128)S(1)}, u32[]{:S(2)}, u32[]{:S(2)}) collective-permute-start(f32[2,32,128]{2,1,0:T(8,128)S(1)} %get-tuple-element.28.yhi), channel_id=1, source_target_pairs={{0,1},{1,2},{2,3},{3,4},{4,5},{5,6},{6,7},{7,8},{8,9},{9,10},{10,1... | collective-permute-start | bytes 98312 | tf_op jit(solution)/shard_map/ppermute | solution.py:288
  13.0 3.6 %copy-start.3 = (f32[32,32,128]{2,1,0:T(8,128)S(1)}, f32[32,32,128]{2,1,0:T(8,128)}, u32[]{:S(2)}) copy-start(f32[32,32,128]{2,1,0:T(8,128)} %param.4) | copy-start | bytes 1572868
  16.5 28.2 %copy-start.1 = (f32[32,32,128]{2,1,0:T(8,128)S(1)}, f32[32,32,128]{2,1,0:T(8,128)}, u32[]{:S(2)}) copy-start(f32[32,32,128]{2,1,0:T(8,128)} %param.3) | copy-start | bytes 1572868

commit v2 on v1

v2 whole, which is shorter than its diff:
```python
import functools

import jax
import jax.numpy as jnp
from jax import lax
from jax.experimental import pallas as pl
from jax.experimental.pallas import tpu as pltpu
from jax.sharding import PartitionSpec as P

COEF_Z = 8.0
COEF_X = 5120.0
COEF_Y = 5120.0

N = 32
L = 128
ROWS = N * N
ROW = 8
VMEM_LIMIT = 24 << 20


def link(coef, one, other):
    return coef * (one * other) / (one + other)


def xp(i):
    return pl.ds(pl.multiple_of(i * N, N), N)


def yp(j):
    return pl.ds(j, N, stride=N)


def zp(z):
    return pl.ds(pl.multiple_of(z * 8, 8), 8)


def halo_planes():
    odd = lax.rem(lax.axis_index("gy"), 2)
    return (1 - odd) * (N - 1), odd * (N - 1)


def pack_kernel(h, k, far, near, sems):
    at_near, at_far = halo_planes()
    copies = [
        pltpu.make_async_copy(src.at[:, at, :], out.at[row], sems.at[2 * side + row])
        for side, (out, at) in enumerate(((far, at_far), (near, at_near)))
        for row, src in enumerate((h, k))
    ]
    for copy in copies:
        copy.start()
    for copy in copies:
        copy.wait()


def chain_step(i, state, e, b_out, e_out, i_out):
    beta, ground, a = state
    inv = 1.0 / (beta + e + ground)
    bh = beta * inv
    eh = e * inv
    b_out[xp(i), :] = bh
    e_out[xp(i), :] = eh
    i_out[xp(i), :] = inv
    return bh * e, 1.0 + eh * ground, a + bh * ground


def local_kernel(h, k, f, bx, ex, ix, mx, by, ey, iy, my, ez, iz, wx, wy, wz, wzt):
    lane = lax.broadcasted_iota(jnp.int32, (N, L), 1)
    row = lax.broadcasted_iota(jnp.int32, (N, L), 0)
    one = jnp.ones((N, L), jnp.float32)

    def flows(i, k0, kn, hn):
        h0 = h[xp(i), :]
        w = jnp.where(row < N - 1, link(COEF_Y, k0, kn), 0.0)
        wy[xp(i), :] = w
        up = 2.0 * w * (hn - h0)
        total = 2.0 * h0 + (up - pltpu.roll(up, 1, 0))
        w = jnp.where(lane < L - 1, link(COEF_Z, k0, pltpu.roll(k0, L - 1, 1)), 0.0)
        wz[xp(i), :] = w
        up = 2.0 * w * (pltpu.roll(h0, L - 1, 1) - h0)
        f[xp(i), :] = total + (up - pltpu.roll(up, 1, 1))

    def further(ref, i):
        return ref[pl.ds(pl.multiple_of(i * N, N) + 1, N), :]

    def plane(i, k0):
        k1 = k[xp(i + 1), :]
        wx[xp(i), :] = link(COEF_X, k0, k1)
        flows(i, k0, further(k, i), further(h, i))
        return k1

    k0 = k[xp(0), :]
    mx[3] = k0
    k1 = lax.fori_loop(0, N - 1, plane, k0, unroll=4)
    mx[4] = k1
    flows(N - 1, k1, pltpu.roll(k1, N - 1, 0), pltpu.roll(h[xp(N - 1), :], N - 1, 0))
    my[3], my[4] = k[yp(0), :], k[yp(N - 1), :]

    for g in range(8):
        wzt[pl.ds(g, L, stride=8), :] = jnp.transpose(wz[pl.ds(g * L, L), :])

    def z_link(i):
        return wzt[zp(i), :]

    def z_step(i, state):
        lo, hi = state
        e = z_link(i)
        inv = 1.0 / (lo + e)
        eh = e * inv
        ez[zp(i), :] = eh
        iz[zp(i), :] = inv
        lo = 1.0 + eh * lo
        t = L - 1 - i
        e = z_link(t - 1)
        inv = 1.0 / (hi + e)
        eh = e * inv
        ez[zp(t), :] = eh
        iz[zp(t), :] = inv
        hi = 1.0 + eh * hi
        return lo, hi

    def chains(i, state):
        sx, sy, sz = state
        sx = chain_step(i, sx, wx[xp(i), :], bx, ex, ix)
        sy = chain_step(i, sy, wy[yp(i), :], by, ey, iy)
        sz = z_step(2 * i - 2, sz)
        sz = z_step(2 * i - 1, sz)
        return sx, sy, sz

    zone = jnp.ones((8, L), jnp.float32)
    sx, sy, sz = lax.fori_loop(
        1, N - 1, chains, ((wx[xp(0), :], one, one), (wy[yp(0), :], one, one), (zone, zone))
    )
    mx[0], mx[2], mx[1] = sx
    my[0], my[2], my[1] = sy
    for i in range(2 * N - 4, 2 * N - 1):
        sz = z_step(i, sz)
    lo, hi = sz
    mid = L // 2 - 1
    e = z_link(mid)
    inv = 1.0 / (hi + e)
    eh = e * inv
    ez[zp(mid + 1), :] = eh
    iz[zp(mid + 1), :] = inv
    iz[zp(mid), :] = 1.0 / (lo + eh * hi)
    ez[zp(mid), :] = jnp.zeros((8, L), jnp.float32)


def send_segment(out, m, s0, s1):
    for at, value in enumerate((m[0], m[1], m[2], s0, s1, m[3], m[4])):
        out[pl.ds(at, N, stride=ROW), :] = value


def x_down_kernel(f, rc, bx, ex, ix, mx, far, near, far_in, near_in, out, s_out, g):
    g[...] = f[...] + rc[...]
    at_near, at_far = halo_planes()
    for at, mine, theirs in ((at_far, far, far_in), (at_near, near, near_in)):
        w = link(COEF_Y, mine[1], theirs[1])
        g[yp(at), :] = g[yp(at), :] + 2.0 * w * (theirs[0] - mine[0])

    def step(i, state):
        s, r = state
        s_out[xp(i), :] = s * ix[xp(i), :]
        return g[xp(i + 1), :] + ex[xp(i), :] * s, r + bx[xp(i), :] * s

    s, r = lax.fori_loop(
        1, N - 1, step, (g[xp(1), :], g[xp(0), :]), unroll=5
    )
    send_segment(out, mx, r, s)


def ends_kernel(chunk, coef, net, out):
    row = lax.broadcasted_iota(jnp.int32, (N, L), 0)

    def before(v, s):
        return jnp.where(row >= s, pltpu.roll(v, s, 0), 0.0)

    def after(v, s):
        return jnp.where(row < N - s, pltpu.roll(v, N - s, 0), 0.0)

    inner, c0, c1, s0, s1, k0, k1 = (net[pl.ds(at, N, stride=ROW), :] for at in range(7))
    w = link(coef, before(k1, chunk), k0)
    inv0 = 1.0 / (w + inner + c0)
    wh, bh = w * inv0, inner * inv0
    beta = w * bh
    ground = c1 + bh * c0 + after(wh * c0, chunk)
    rhs = s1 + bh * s0 + after(wh * s0, chunk)
    s = chunk
    while s < N:
        nxt = after(beta, s)
        inv = 1.0 / (ground + beta + nxt)
        gh, rh, lh = ground * inv, rhs * inv, beta * inv
        ground = ground + beta * before(gh, s) + nxt * after(gh, s)
        rhs = rhs + beta * before(rh, s) + nxt * after(rh, s)
        beta = beta * before(lh, s)
        s *= 2
    q = rhs / ground
    out[pl.ds(0, N, stride=2), :] = s0 * inv0 + wh * before(q, chunk) + bh * q
    out[pl.ds(1, N, stride=2), :] = q


def x_up_kernel(ends, s_in, bx, ex, h, by, ey, iy, my, out, s_out, d):
    first = ends[pl.ds(0, N, stride=2), :]
    last = ends[pl.ds(1, N, stride=2), :]
    d[xp(N - 1), :] = last - 2.0 * h[xp(N - 1), :]
    d[xp(0), :] = first - 2.0 * h[xp(0), :]

    def back(t, nxt):
        i = N - 1 - t
        cur = (s_in[xp(i), :] + bx[xp(i), :] * first) + ex[xp(i), :] * nxt
        d[xp(i), :] = cur - 2.0 * h[xp(i), :]
        return cur

    lax.fori_loop(1, N - 1, back, last, unroll=5)

    def step(i, state):
        s, r = state
        s_out[xp(i), :] = s * iy[xp(i), :]
        return d[yp(i + 1), :] + ey[xp(i), :] * s, r + by[xp(i), :] * s

    s, r = lax.fori_loop(1, N - 1, step, (d[yp(1), :], d[yp(0), :]), unroll=5)
    send_segment(out, my, r, s)


def final_kernel(ends, s_in, by, ey, ez, iz, h, out, d, t, sems):
    first = ends[pl.ds(0, N, stride=2), :]
    last = ends[pl.ds(1, N, stride=2), :]
    d[xp(N - 1), :] = last
    d[xp(0), :] = first

    def back(u, nxt):
        j = N - 1 - u
        cur = (s_in[xp(j), :] + by[xp(j), :] * first) + ey[xp(j), :] * nxt
        d[xp(j), :] = cur
        return cur

    lax.fori_loop(1, N - 1, back, last, unroll=5)

    for g in range(8):
        lines = jnp.concatenate([d[yp(i), :] for i in range(4 * g, 4 * g + 4)])
        t[pl.ds(g, L, stride=8), :] = jnp.transpose(lines)

    mid = L // 2 - 1

    def down(i, state):
        lo, hi = state
        u = L - 1 - i
        t[zp(i), :] = lo * iz[zp(i), :]
        t[zp(u), :] = hi * iz[zp(u), :]
        return t[zp(i + 1), :] + ez[zp(i), :] * lo, t[zp(u - 1), :] + ez[zp(u), :] * hi

    lo, hi = lax.fori_loop(0, mid, down, (t[zp(0), :], t[zp(L - 1), :]), unroll=9)
    t[zp(mid + 1), :] = hi * iz[zp(mid + 1), :]
    m = (lo + ez[zp(mid + 1), :] * hi) * iz[zp(mid), :]
    t[zp(mid), :] = m
    hi = t[zp(mid + 1), :] + ez[zp(mid + 1), :] * m
    t[zp(mid + 1), :] = hi

    def up(i, state):
        lo, hi = state
        a = mid - i
        b = mid + 1 + i
        lo = t[zp(a), :] + ez[zp(a), :] * lo
        hi = t[zp(b), :] + ez[zp(b), :] * hi
        t[zp(a), :] = lo
        t[zp(b), :] = hi
        return lo, hi

    lax.fori_loop(1, mid + 1, up, (m, hi), unroll=9)
    copies = []
    for g in range(8):
        at = pl.ds(g * L, L)
        d[at, :] = h[at, :] + jnp.transpose(t[pl.ds(g, L, stride=8), :])
        copies.append(pltpu.make_async_copy(d.at[at, :], out.at[at, :], sems.at[g]))
        copies[g].start()
    for copy in copies:
        copy.wait()


BLOCK = (ROWS, L)
NET = (N * ROW, L)
ENDS = (N * 2, L)


def planes(*lead):
    return lead + (N, L)


def call(kernel, outs, *args, scratch=(), sems=0, hbm_in=(), hbm_out=False, flops=1000000):
    spec = {True: pl.BlockSpec(memory_space=pltpu.HBM), False: pl.BlockSpec(memory_space=pltpu.VMEM)}
    moved = 4 * sum(a.size for a in args)
    args = [
        pltpu.with_memory_space_constraint(a, pltpu.HBM if i in hbm_in else pltpu.VMEM)
        for i, a in enumerate(args)
    ]
    make = jax.ShapeDtypeStruct if hbm_out else pltpu.VMEM
    scratch_shapes = [pltpu.VMEM(s, jnp.float32) for s in scratch]
    if sems:
        scratch_shapes.append(pltpu.SemaphoreType.DMA((sems,)))
    return pl.pallas_call(
        kernel,
        out_shape=[make(s, jnp.float32) for s in outs],
        in_specs=[spec[i in hbm_in] for i in range(len(args))],
        out_specs=[spec[hbm_out]] * len(outs),
        scratch_shapes=scratch_shapes,
        compiler_params=pltpu.CompilerParams(vmem_limit_bytes=VMEM_LIMIT),
        cost_estimate=pl.CostEstimate(flops=flops, bytes_accessed=moved, transcendentals=0),
    )(*args)


def line_ends(net, axis, coef):
    chunk = N // lax.axis_size(axis)
    got = lax.all_to_all(net.reshape(N, ROW, L), axis, 0, 0, tiled=True).reshape(NET)
    (ends,) = call(functools.partial(ends_kernel, chunk, coef), [ENDS], got, flops=100000)
    return lax.all_to_all(ends.reshape(N, 2, L), axis, 0, 0, tiled=True).reshape(ENDS)


def per_device(water_head, conductivity, recharge):
    h, k, rc = (a.reshape(ROWS, L) for a in (water_head, conductivity, recharge))
    far, near = call(
        pack_kernel, [planes(2)] * 2, water_head, conductivity, sems=4, hbm_in=(0, 1), flops=10000
    )
    count = lax.axis_size("gy")
    across = [(i, i + 1) for i in range(1, count - 1, 2)]
    far_in = lax.ppermute(far, "gy", across + [(i, j) for j, i in across])
    near_in = lax.ppermute(near, "gy", [(i, i ^ 1) for i in range(count)])
    f, bx, ex, ix, mx, by, ey, iy, my, ez, iz = call(
        local_kernel,
        [BLOCK] * 4 + [planes(5)] + [BLOCK] * 3 + [planes(5)] + [BLOCK] * 2,
        h, k,
        scratch=[BLOCK] * 4,
        flops=20000000,
    )
    net, sx = call(
        x_down_kernel,
        [NET, BLOCK],
        f, rc, bx, ex, ix, mx, far, near, far_in, near_in,
        scratch=[BLOCK],
    )
    ends = line_ends(net, "gx", COEF_X)
    net, sy = call(x_up_kernel, [NET, BLOCK], ends, sx, bx, ex, h, by, ey, iy, my, scratch=[BLOCK])
    ends = line_ends(net, "gy", COEF_Y)
    (out,) = call(
        final_kernel, [BLOCK], ends, sy, by, ey, ez, iz, h, hbm_out=True, scratch=[BLOCK] * 2, sems=8
    )
    return out.reshape(water_head.shape)


def solution(mesh):
    placed = (P("gx", "gy", None),) * 3
    return jax.shard_map(
        per_device, mesh=mesh, in_specs=placed, out_specs=P("gx", "gy", None), check_vma=False
    )
```

time: 79.2 us -> 77 us (0.972)
  local copies, waits for them, and re-layouts: 2.1 us -> 0.01 us
  starting transfers between devices: 10.8 us -> 9.41 us
  blocking collectives: 58.8 us -> 60.1 us
    unnamed x10 -> x6, local copies, waits for them, and re-layouts: 2.1 us -> 0.01 us
    ppermute x2, starting transfers between devices: 10.8 us -> 9.41 us  [the longest x1 5.38 us: per_device(): far_in = lax.ppermute(far, 'gy', across + [(i, j) for j, i in across])]
    all_to_all x2, blocking collectives: 37 us -> 37.8 us  [line_ends(): lax.all_to_all(net.reshape(N, ROW, L), axis, 0, 0, tiled=True).reshape(NET)]
where the time goes in v2:
time: 77 us; the launch traced here: 76.7 us
  blocking collectives  60.1 us (78%)
  starting transfers between devices  9.41 us (12%)
  Pallas kernels  7.1 us (9%)
    all_to_all x2, blocking collectives, line_ends(): lax.all_to_all(net.reshape(N, ROW, L), axis, 0, 0, tiled=True).reshape(NET)  37.8 us
    all_to_all x2, blocking collectives, line_ends(): lax.all_to_all(ends.reshape(N, 2, L), axis, 0, 0, tiled=True).reshape(ENDS)  22.3 us
    pallas_call x7, Pallas kernels, call(): pl.pallas_call(kernel, out_shape=[make(s, jnp.float32) for s in outs], in...  7.1 us
    ppermute x1, starting transfers between devices, per_device(): far_in = lax.ppermute(far, 'gy', across + [(i, j) for j, i in across])  5.38 us
    ppermute x1, starting transfers between devices, per_device(): near_in = lax.ppermute(near, 'gy', [(i, i ^ 1) for i in range(count)])  4.03 us
  transfers between devices with their start and end apart: 2, of which 0 were waited for; matrix products, arithmetic and copies ran while one was open for 0% of the time, Pallas kernels for 4%

profile of v2, /device:TPU:1, one launch (start us, length us, event | category | flops | bytes accessed | tf_op | source)
XLA Modules:
  0.0 76.7 jit_solution(1095313774522215577)
XLA Ops:
  0.0 0.0 copy-start.1
  0.0 0.0 copy-start
  0.0 0.9 %shard_map.38 = (f32[2,32,128]{2,1,0:T(8,128)S(1)}, f32[2,32,128]{2,1,0:T(8,128)S(1)}) custom-call(f32[32,32,128]{2,1,0:T(8,128)} %h.1, f32[32,32,128]{2,1,0:T(8,128)} %k.1), custom_call_target="tpu_custom_call" | custom-call | flops 10000 | bytes 1048576 | tf_op jit(solution)/shard_map/pallas_call | solution.py:299
  0.9 5.4 %collective-permute-start = (f32[2,32,128]{2,1,0:T(8,128)S(1)}, f32[2,32,128]{2,1,0:T(8,128)S(1)}, u32[]{:S(2)}, u32[]{:S(2)}) collective-permute-start(f32[2,32,128]{2,1,0:T(8,128)S(1)} %get-tuple-element.27.far), channel_id=1, source_target_pairs={{1,2},{3,4},{5,6},{7,8},{9,10},{11,12},{13,14},{2,1},{4,3},{6,5},{... | collective-permute-start | bytes 98312 | tf_op jit(solution)/shard_map/ppermute | solution.py:324
  6.3 4.0 %collective-permute-start.1 = (f32[2,32,128]{2,1,0:T(8,128)S(1)}, f32[2,32,128]{2,1,0:T(8,128)S(1)}, u32[]{:S(2)}, u32[]{:S(2)}) collective-permute-start(f32[2,32,128]{2,1,0:T(8,128)S(1)} %get-tuple-element.28.near), channel_id=1, source_target_pairs={{0,1},{1,0},{2,3},{3,2},{4,5},{5,4},{6,7},{7,6},{8,9},{9,8},{10,11... | collective-permute-start | bytes 98312 | tf_op jit(solution)/shard_map/ppermute | solution.py:325
  10.3 0.0 copy-done.1
  10.3 0.0 copy-done
  10.3 0.0 copy-start.2
  10.4 3.1 %shard_map.37 = (f32[1024,128]{1,0:T(8,128)S(1)}, f32[1024,128]{1,0:T(8,128)S(1)}, f32[1024,128]{1,0:T(8,128)S(1)}, f32[1024,128]{1,0:T(8,128)S(1)}, f32[5,32,12...) custom-call(f32[1024,128]{1,0:T(8,128)S(1)} %bitcast.12, ...), custom_call_target="tpu_custom_call" | custom-call | flops 20000000 | bytes 1048576 | tf_op jit(solution)/shard_map/pallas_call | solution.py:299
  13.4 0.0 collective-permute-done.far_in
  13.5 0.0 collective-permute-done.1.near_in
  13.5 0.0 copy-done.2
  13.5 0.2 shard_map.39
  13.7 16.7 %all_to_all.20 = f32[32,8,128]{2,1,0:T(8,128)S(1)} all-to-all(f32[32,8,128]{2,1,0:T(8,128)S(1)} %bitcast.22), channel_id=1, replica_groups=mesh['gx'=32,'gy'=16] {'gx'}, dimensions={0} | all-to-all | bytes 262144 | tf_op jit(solution)/shard_map/all_to_all | solution.py:312
  30.4 0.1 shard_map.40
  30.6 12.2 %all_to_all.21 = f32[32,2,128]{2,1,0:T(2,128)S(1)} all-to-all(f32[32,2,128]{2,1,0:T(2,128)S(1)} %bitcast.20), channel_id=1, replica_groups=mesh['gx'=32,'gy'=16] {'gx'}, dimensions={0} | all-to-all | bytes 65536 | tf_op jit(solution)/shard_map/all_to_all | solution.py:314
  42.8 0.6 shard_map.41
  43.4 21.1 %all_to_all.22 = f32[32,8,128]{2,1,0:T(8,128)S(1)} all-to-all(f32[32,8,128]{2,1,0:T(8,128)S(1)} %bitcast.23), channel_id=1, replica_groups=mesh['gx'=32,'gy'=16] {'gy'}, dimensions={0} | all-to-all | bytes 262144 | tf_op jit(solution)/shard_map/all_to_all | solution.py:312
  64.5 0.1 shard_map.42
  64.6 10.1 %all_to_all.23 = f32[32,2,128]{2,1,0:T(2,128)S(1)} all-to-all(f32[32,2,128]{2,1,0:T(2,128)S(1)} %bitcast.21), channel_id=1, replica_groups=mesh['gx'=32,'gy'=16] {'gy'}, dimensions={0} | all-to-all | bytes 65536 | tf_op jit(solution)/shard_map/all_to_all | solution.py:314
  74.7 2.1 %shard_map.43 = f32[1024,128]{1,0:T(8,128)} custom-call(f32[64,128]{1,0:T(8,128)S(1)} %bitcast.19, f32[1024,128]{1,0:T(8,128)S(1)} %get-tuple-element.36.s_in, f32[1024,128]{1,0:T(8,128)S(1)} %get-tuple-element.31.by, f32[1024,128]{1,0:T(8,128)S(1)} %get-tuple-element.32.ey, f32[1024,128]{1,0:T(8,128)S(1)} %get-tuple-element.37.ez, ...), custom_call_target="tpu_custom_call" | custom-call | flops 1000000 | bytes 3178496 | tf_op jit(solution)/shard_map/pallas_call | solution.py:299
Async XLA Ops:
  0.0 10.3 %copy-start.1 = (f32[32,32,128]{2,1,0:T(8,128)S(1)}, f32[32,32,128]{2,1,0:T(8,128)}, u32[]{:S(2)}) copy-start(f32[32,32,128]{2,1,0:T(8,128)} %k.1) | copy-start | bytes 1572868
  0.0 10.3 %copy-start = (f32[32,32,128]{2,1,0:T(8,128)S(1)}, f32[32,32,128]{2,1,0:T(8,128)}, u32[]{:S(2)}) copy-start(f32[32,32,128]{2,1,0:T(8,128)} %h.1) | copy-start | bytes 1572868
  0.9 12.5 %collective-permute-start = (f32[2,32,128]{2,1,0:T(8,128)S(1)}, f32[2,32,128]{2,1,0:T(8,128)S(1)}, u32[]{:S(2)}, u32[]{:S(2)}) collective-permute-start(f32[2,32,128]{2,1,0:T(8,128)S(1)} %get-tuple-element.27.far), channel_id=1, source_target_pairs={{1,2},{3,4},{5,6},{7,8},{9,10},{11,12},{13,14},{2,1},{4,3},{6,5},{... | collective-permute-start | bytes 98312 | tf_op jit(solution)/shard_map/ppermute | solution.py:324
  6.3 7.2 %collective-permute-start.1 = (f32[2,32,128]{2,1,0:T(8,128)S(1)}, f32[2,32,128]{2,1,0:T(8,128)S(1)}, u32[]{:S(2)}, u32[]{:S(2)}) collective-permute-start(f32[2,32,128]{2,1,0:T(8,128)S(1)} %get-tuple-element.28.near), channel_id=1, source_target_pairs={{0,1},{1,0},{2,3},{3,2},{4,5},{5,4},{6,7},{7,6},{8,9},{9,8},{10,11... | collective-permute-start | bytes 98312 | tf_op jit(solution)/shard_map/ppermute | solution.py:325
  10.3 3.1 %copy-start.2 = (f32[32,32,128]{2,1,0:T(8,128)S(1)}, f32[32,32,128]{2,1,0:T(8,128)}, u32[]{:S(2)}) copy-start(f32[32,32,128]{2,1,0:T(8,128)} %param.5) | copy-start | bytes 1572868

commit v3 on v2

--- a/solution.py
+++ b/solution.py
@@ -15,6 +15,8 @@
 L = 128
 ROWS = N * N
 ROW = 8
+LAST = L // 2 - 1
+MID = LAST // 2
 VMEM_LIMIT = 24 << 20
 
 
@@ -63,20 +65,22 @@
     return bh * e, 1.0 + eh * ground, a + bh * ground
 
 
-def local_kernel(h, k, f, bx, ex, ix, mx, by, ey, iy, my, ez, iz, wx, wy, wz, wzt):
+def local_kernel(h, k, f, bx, ex, ix, mx, by, ey, iy, my, zb, ze, zi, ez, iz, wx, wy, wz, wzt):
     lane = lax.broadcasted_iota(jnp.int32, (N, L), 1)
     row = lax.broadcasted_iota(jnp.int32, (N, L), 0)
     one = jnp.ones((N, L), jnp.float32)
+    coef_y = jnp.where(row < N - 1, COEF_Y, 0.0)
+    coef_z = jnp.where(lane < L - 1, COEF_Z, 0.0)
 
     def flows(i, k0, kn, hn):
-        h0 = h[xp(i), :]
-        w = jnp.where(row < N - 1, link(COEF_Y, k0, kn), 0.0)
+        h0 = 2.0 * h[xp(i), :]
+        w = link(coef_y, k0, kn)
         wy[xp(i), :] = w
-        up = 2.0 * w * (hn - h0)
-        total = 2.0 * h0 + (up - pltpu.roll(up, 1, 0))
-        w = jnp.where(lane < L - 1, link(COEF_Z, k0, pltpu.roll(k0, L - 1, 1)), 0.0)
+        up = w * (2.0 * hn - h0)
+        total = h0 + (up - pltpu.roll(up, 1, 0))
+        w = link(coef_z, k0, pltpu.roll(k0, L - 1, 1))
         wz[xp(i), :] = w
-        up = 2.0 * w * (pltpu.roll(h0, L - 1, 1) - h0)
+        up = w * (pltpu.roll(h0, L - 1, 1) - h0)
         f[xp(i), :] = total + (up - pltpu.roll(up, 1, 1))
 
     def further(ref, i):
@@ -90,7 +94,7 @@
 
     k0 = k[xp(0), :]
     mx[3] = k0
-    k1 = lax.fori_loop(0, N - 1, plane, k0, unroll=4)
+    k1 = lax.fori_loop(1, N - 1, plane, plane(0, k0), unroll=5)
     mx[4] = k1
     flows(N - 1, k1, pltpu.roll(k1, N - 1, 0), pltpu.roll(h[xp(N - 1), :], N - 1, 0))
     my[3], my[4] = k[yp(0), :], k[yp(N - 1), :]
@@ -98,51 +102,49 @@
     for g in range(8):
         wzt[pl.ds(g, L, stride=8), :] = jnp.transpose(wz[pl.ds(g * L, L), :])
 
-    def z_link(i):
-        return wzt[zp(i), :]
-
-    def z_step(i, state):
-        lo, hi = state
-        e = z_link(i)
-        inv = 1.0 / (lo + e)
-        eh = e * inv
-        ez[zp(i), :] = eh
-        iz[zp(i), :] = inv
-        lo = 1.0 + eh * lo
-        t = L - 1 - i
-        e = z_link(t - 1)
-        inv = 1.0 / (hi + e)
-        eh = e * inv
-        ez[zp(t), :] = eh
-        iz[zp(t), :] = inv
-        hi = 1.0 + eh * hi
-        return lo, hi
+    def odd_cell(m):
+        w0 = wzt[zp(2 * m), :]
+        w1 = wzt[zp(2 * m + 1), :]
+        inv = 1.0 / (1.0 + w0 + w1)
+        b = w0 * inv
+        e = w1 * inv
+        zb[zp(m), :] = b
+        ze[zp(m), :] = e
+        zi[zp(m), :] = inv
+        return b, e, b * w1
+
+    def even_cell(m, ground, past):
+        inv = 1.0 / (ground + past)
+        eh = past * inv
+        ez[zp(m), :] = eh
+        iz[zp(m), :] = inv
+        return eh * ground
+
+    def z_step(q, state):
+        lo, (b0, e0, w0), o1, hi, p0, p1 = state
+        lo = (1.0 + e0 + o1[0]) + even_cell(q, lo, w0)
+        hi = (1.0 + p0[0] + p1[1]) + even_cell(LAST - q, hi, p0[2])
+        return lo, o1, odd_cell(q + 2), hi, p1, odd_cell(LAST - 3 - q)
 
     def chains(i, state):
         sx, sy, sz = state
         sx = chain_step(i, sx, wx[xp(i), :], bx, ex, ix)
         sy = chain_step(i, sy, wy[yp(i), :], by, ey, iy)
-        sz = z_step(2 * i - 2, sz)
-        sz = z_step(2 * i - 1, sz)
-        return sx, sy, sz
-
-    zone = jnp.ones((8, L), jnp.float32)
+        return sx, sy, z_step(i - 1, sz)
+
+    o0, o1 = odd_cell(0), odd_cell(1)
+    top, p0, p1 = odd_cell(LAST), odd_cell(LAST - 1), odd_cell(LAST - 2)
+    sz = (1.0 + o0[0], o0, o1, 1.0 + top[0] + p0[1], p0, p1)
     sx, sy, sz = lax.fori_loop(
-        1, N - 1, chains, ((wx[xp(0), :], one, one), (wy[yp(0), :], one, one), (zone, zone))
+        1, N - 1, chains, ((wx[xp(0), :], one, one), (wy[yp(0), :], one, one), sz), unroll=3
     )
     mx[0], mx[2], mx[1] = sx
     my[0], my[2], my[1] = sy
-    for i in range(2 * N - 4, 2 * N - 1):
-        sz = z_step(i, sz)
-    lo, hi = sz
-    mid = L // 2 - 1
-    e = z_link(mid)
-    inv = 1.0 / (hi + e)
-    eh = e * inv
-    ez[zp(mid + 1), :] = eh
-    iz[zp(mid + 1), :] = inv
-    iz[zp(mid), :] = 1.0 / (lo + eh * hi)
-    ez[zp(mid), :] = jnp.zeros((8, L), jnp.float32)
+    lo, (b0, e0, w0), o1, hi, p0, p1 = sz
+    lo = (1.0 + e0 + o1[0]) + even_cell(MID - 1, lo, w0)
+    hi = (1.0 + p0[0] + p1[1]) + even_cell(MID + 2, hi, p0[2])
+    lo = lo + even_cell(MID + 1, hi, p1[2])
+    iz[zp(MID), :] = 1.0 / lo
 
 
 def send_segment(out, m, s0, s1):
@@ -210,18 +212,18 @@
         d[xp(i), :] = cur - 2.0 * h[xp(i), :]
         return cur
 
-    lax.fori_loop(1, N - 1, back, last, unroll=5)
+    lax.fori_loop(1, N - 1, back, last, unroll=10)
 
     def step(i, state):
         s, r = state
         s_out[xp(i), :] = s * iy[xp(i), :]
         return d[yp(i + 1), :] + ey[xp(i), :] * s, r + by[xp(i), :] * s
 
-    s, r = lax.fori_loop(1, N - 1, step, (d[yp(1), :], d[yp(0), :]), unroll=5)
+    s, r = lax.fori_loop(1, N - 1, step, (d[yp(1), :], d[yp(0), :]), unroll=10)
     send_segment(out, my, r, s)
 
 
-def final_kernel(ends, s_in, by, ey, ez, iz, h, out, d, t, sems):
+def final_kernel(ends, s_in, by, ey, zb, ze, zi, ez, iz, h, out, d, t, sems):
     first = ends[pl.ds(0, N, stride=2), :]
     last = ends[pl.ds(1, N, stride=2), :]
     d[xp(N - 1), :] = last
@@ -233,39 +235,52 @@
         d[xp(j), :] = cur
         return cur
 
-    lax.fori_loop(1, N - 1, back, last, unroll=5)
+    lax.fori_loop(1, N - 1, back, last, unroll=10)
 
     for g in range(8):
         lines = jnp.concatenate([d[yp(i), :] for i in range(4 * g, 4 * g + 4)])
         t[pl.ds(g, L, stride=8), :] = jnp.transpose(lines)
 
-    mid = L // 2 - 1
-
-    def down(i, state):
+    def reduced(m):
+        return (t[zp(2 * m), :] + zb[zp(m), :] * t[zp(2 * m + 1), :]) + ze[zp(m - 1), :] * t[zp(2 * m - 1), :]
+
+    def down(q, state):
         lo, hi = state
-        u = L - 1 - i
-        t[zp(i), :] = lo * iz[zp(i), :]
-        t[zp(u), :] = hi * iz[zp(u), :]
-        return t[zp(i + 1), :] + ez[zp(i), :] * lo, t[zp(u - 1), :] + ez[zp(u), :] * hi
-
-    lo, hi = lax.fori_loop(0, mid, down, (t[zp(0), :], t[zp(L - 1), :]), unroll=9)
-    t[zp(mid + 1), :] = hi * iz[zp(mid + 1), :]
-    m = (lo + ez[zp(mid + 1), :] * hi) * iz[zp(mid), :]
-    t[zp(mid), :] = m
-    hi = t[zp(mid + 1), :] + ez[zp(mid + 1), :] * m
-    t[zp(mid + 1), :] = hi
-
-    def up(i, state):
+        m = LAST - q
+        next_lo = reduced(q + 1) + ez[zp(q), :] * lo
+        next_hi = reduced(m - 1) + ez[zp(m), :] * hi
+        t[zp(2 * q), :] = lo * iz[zp(q), :]
+        t[zp(2 * m), :] = hi * iz[zp(m), :]
+        return next_lo, next_hi
+
+    lo, hi = t[zp(0), :] + zb[zp(0), :] * t[zp(1), :], reduced(LAST)
+    lo, hi = lax.fori_loop(0, MID, down, (lo, hi), unroll=31)
+    mid = (lo + ez[zp(MID + 1), :] * hi) * iz[zp(MID), :]
+    t[zp(2 * MID), :] = mid
+    t[zp(2 * MID + 2), :] = hi * iz[zp(MID + 1), :]
+
+    def odd_back(m, below, above):
+        at = zp(2 * m + 1)
+        t[at, :] = (zi[zp(m), :] * t[at, :] + zb[zp(m), :] * below) + ze[zp(m), :] * above
+
+    def up(q, state):
         lo, hi = state
-        a = mid - i
-        b = mid + 1 + i
-        lo = t[zp(a), :] + ez[zp(a), :] * lo
-        hi = t[zp(b), :] + ez[zp(b), :] * hi
-        t[zp(a), :] = lo
-        t[zp(b), :] = hi
-        return lo, hi
-
-    lax.fori_loop(1, mid + 1, up, (m, hi), unroll=9)
+        a = MID - 1 - q
+        b = MID + 1 + q
+        next_lo = t[zp(2 * a), :] + ez[zp(a), :] * lo
+        next_hi = t[zp(2 * b), :] + ez[zp(b), :] * hi
+        t[zp(2 * a), :] = next_lo
+        t[zp(2 * b), :] = next_hi
+        odd_back(a, next_lo, lo)
+        odd_back(b - 1, hi, next_hi)
+        return next_lo, next_hi
+
+    lo, hi = lax.fori_loop(0, MID, up, (mid, mid), unroll=31)
+    next_hi = t[zp(2 * LAST), :] + ez[zp(LAST), :] * hi
+    t[zp(2 * LAST), :] = next_hi
+    odd_back(LAST - 1, hi, next_hi)
+    odd_back(LAST, next_hi, 0.0)
+
     copies = []
     for g in range(8):
         at = pl.ds(g * L, L)
@@ -277,6 +292,7 @@
 
 
 BLOCK = (ROWS, L)
+HALF = (ROWS // 2, L)
 NET = (N * ROW, L)
 ENDS = (N * 2, L)
 
@@ -323,9 +339,9 @@
     across = [(i, i + 1) for i in range(1, count - 1, 2)]
     far_in = lax.ppermute(far, "gy", across + [(i, j) for j, i in across])
     near_in = lax.ppermute(near, "gy", [(i, i ^ 1) for i in range(count)])
-    f, bx, ex, ix, mx, by, ey, iy, my, ez, iz = call(
+    f, bx, ex, ix, mx, by, ey, iy, my, *z = call(
         local_kernel,
-        [BLOCK] * 4 + [planes(5)] + [BLOCK] * 3 + [planes(5)] + [BLOCK] * 2,
+        [BLOCK] * 4 + [planes(5)] + [BLOCK] * 3 + [planes(5)] + [HALF] * 5,
         h, k,
         scratch=[BLOCK] * 4,
         flops=20000000,
@@ -340,7 +356,7 @@
     net, sy = call(x_up_kernel, [NET, BLOCK], ends, sx, bx, ex, h, by, ey, iy, my, scratch=[BLOCK])
     ends = line_ends(net, "gy", COEF_Y)
     (out,) = call(
-        final_kernel, [BLOCK], ends, sy, by, ey, ez, iz, h, hbm_out=True, scratch=[BLOCK] * 2, sems=8
+        final_kernel, [BLOCK], ends, sy, by, ey, *z, h, hbm_out=True, scratch=[BLOCK] * 2, sems=8
     )
     return out.reshape(water_head.shape)
 

time: 77 us -> 75.8 us (0.984)
  Pallas kernels: 7.1 us -> 5.88 us
    pallas_call x7, Pallas kernels: 7.1 us -> 5.88 us  [call(): pl.pallas_call(kernel, out_shape=[make(s, jnp.float32) for s in outs], in...]
  transfers between devices with their start and end apart: 2 -> 2, of which waited for: 0 -> 0; matrix products, arithmetic and copies ran while one was open for 0% -> 0% of each run, Pallas kernels for 4% -> 3%
where the time goes in v3:
time: 75.8 us; the launch traced here: 75.5 us
  blocking collectives  60.1 us (79%)
  starting transfers between devices  9.41 us (12%)
  Pallas kernels  5.88 us (8%)
    all_to_all x2, blocking collectives, line_ends(): lax.all_to_all(net.reshape(N, ROW, L), axis, 0, 0, tiled=True).reshape(NET)  37.8 us
    all_to_all x2, blocking collectives, line_ends(): lax.all_to_all(ends.reshape(N, 2, L), axis, 0, 0, tiled=True).reshape(ENDS)  22.3 us
    pallas_call x7, Pallas kernels, call(): pl.pallas_call(kernel, out_shape=[make(s, jnp.float32) for s in outs], in...  5.88 us
    ppermute x1, starting transfers between devices, per_device(): far_in = lax.ppermute(far, 'gy', across + [(i, j) for j, i in across])  5.38 us
    ppermute x1, starting transfers between devices, per_device(): near_in = lax.ppermute(near, 'gy', [(i, i ^ 1) for i in range(count)])  4.03 us
  transfers between devices with their start and end apart: 2, of which 0 were waited for; matrix products, arithmetic and copies ran while one was open for 0% of the time, Pallas kernels for 3%

profile of v3, /device:TPU:1, one launch (start us, length us, event | category | flops | bytes accessed | tf_op | source)
XLA Modules:
  0.0 75.5 jit_solution(17971207566388733593)
XLA Ops:
  0.0 0.0 copy-start.1
  0.0 0.0 copy-start
  0.0 0.9 %shard_map.38 = (f32[2,32,128]{2,1,0:T(8,128)S(1)}, f32[2,32,128]{2,1,0:T(8,128)S(1)}) custom-call(f32[32,32,128]{2,1,0:T(8,128)} %h.1, f32[32,32,128]{2,1,0:T(8,128)} %k.1), custom_call_target="tpu_custom_call" | custom-call | flops 10000 | bytes 1048576 | tf_op jit(solution)/shard_map/pallas_call | solution.py:315
  0.9 5.4 %collective-permute-start = (f32[2,32,128]{2,1,0:T(8,128)S(1)}, f32[2,32,128]{2,1,0:T(8,128)S(1)}, u32[]{:S(2)}, u32[]{:S(2)}) collective-permute-start(f32[2,32,128]{2,1,0:T(8,128)S(1)} %get-tuple-element.30.far), channel_id=1, source_target_pairs={{1,2},{3,4},{5,6},{7,8},{9,10},{11,12},{13,14},{2,1},{4,3},{6,5},{... | collective-permute-start | bytes 98312 | tf_op jit(solution)/shard_map/ppermute | solution.py:340
  6.3 4.0 %collective-permute-start.1 = (f32[2,32,128]{2,1,0:T(8,128)S(1)}, f32[2,32,128]{2,1,0:T(8,128)S(1)}, u32[]{:S(2)}, u32[]{:S(2)}) collective-permute-start(f32[2,32,128]{2,1,0:T(8,128)S(1)} %get-tuple-element.31.near), channel_id=1, source_target_pairs={{0,1},{1,0},{2,3},{3,2},{4,5},{5,4},{6,7},{7,6},{8,9},{9,8},{10,11... | collective-permute-start | bytes 98312 | tf_op jit(solution)/shard_map/ppermute | solution.py:341
  10.3 0.0 copy-done.1
  10.3 0.0 copy-done
  10.3 0.0 copy-start.2
  10.4 2.4 %shard_map.37 = (f32[1024,128]{1,0:T(8,128)S(1)}, f32[1024,128]{1,0:T(8,128)S(1)}, f32[1024,128]{1,0:T(8,128)S(1)}, f32[1024,128]{1,0:T(8,128)S(1)}, f32[5,32,12...) custom-call(f32[1024,128]{1,0:T(8,128)S(1)} %bitcast.12, ...), custom_call_target="tpu_custom_call" | custom-call | flops 20000000 | bytes 1048576 | tf_op jit(solution)/shard_map/pallas_call | solution.py:315
  12.7 0.0 collective-permute-done.far_in
  12.7 0.0 collective-permute-done.1.near_in
  12.8 0.0 copy-done.2
  12.8 0.2 shard_map.39
  13.0 16.7 %all_to_all.20 = f32[32,8,128]{2,1,0:T(8,128)S(1)} all-to-all(f32[32,8,128]{2,1,0:T(8,128)S(1)} %bitcast.22), channel_id=1, replica_groups=mesh['gx'=32,'gy'=16] {'gx'}, dimensions={0} | all-to-all | bytes 262144 | tf_op jit(solution)/shard_map/all_to_all | solution.py:328
  29.7 0.1 shard_map.40
  29.8 12.2 %all_to_all.21 = f32[32,2,128]{2,1,0:T(2,128)S(1)} all-to-all(f32[32,2,128]{2,1,0:T(2,128)S(1)} %bitcast.20), channel_id=1, replica_groups=mesh['gx'=32,'gy'=16] {'gx'}, dimensions={0} | all-to-all | bytes 65536 | tf_op jit(solution)/shard_map/all_to_all | solution.py:330
  42.1 0.6 shard_map.41
  42.6 21.1 %all_to_all.22 = f32[32,8,128]{2,1,0:T(8,128)S(1)} all-to-all(f32[32,8,128]{2,1,0:T(8,128)S(1)} %bitcast.23), channel_id=1, replica_groups=mesh['gx'=32,'gy'=16] {'gy'}, dimensions={0} | all-to-all | bytes 262144 | tf_op jit(solution)/shard_map/all_to_all | solution.py:328
  63.7 0.1 shard_map.42
  63.8 10.1 %all_to_all.23 = f32[32,2,128]{2,1,0:T(2,128)S(1)} all-to-all(f32[32,2,128]{2,1,0:T(2,128)S(1)} %bitcast.21), channel_id=1, replica_groups=mesh['gx'=32,'gy'=16] {'gy'}, dimensions={0} | all-to-all | bytes 65536 | tf_op jit(solution)/shard_map/all_to_all | solution.py:330
  73.9 1.6 %shard_map.43 = f32[1024,128]{1,0:T(8,128)} custom-call(f32[64,128]{1,0:T(8,128)S(1)} %bitcast.19, f32[1024,128]{1,0:T(8,128)S(1)} %get-tuple-element.39.s_in, f32[1024,128]{1,0:T(8,128)S(1)} %get-tuple-element.34.by, f32[1024,128]{1,0:T(8,128)S(1)} %get-tuple-element.35.ey, f32[512,128]{1,0:T(8,128)S(1)} %get-tuple-element.40.zb, ...), custom_call_target="tpu_custom_call" | custom-call | flops 1000000 | bytes 3440640 | tf_op jit(solution)/shard_map/pallas_call | solution.py:315
Async XLA Ops:
  0.0 10.3 %copy-start.1 = (f32[32,32,128]{2,1,0:T(8,128)S(1)}, f32[32,32,128]{2,1,0:T(8,128)}, u32[]{:S(2)}) copy-start(f32[32,32,128]{2,1,0:T(8,128)} %k.1) | copy-start | bytes 1572868
  0.0 10.3 %copy-start = (f32[32,32,128]{2,1,0:T(8,128)S(1)}, f32[32,32,128]{2,1,0:T(8,128)}, u32[]{:S(2)}) copy-start(f32[32,32,128]{2,1,0:T(8,128)} %h.1) | copy-start | bytes 1572868
  0.9 11.8 %collective-permute-start = (f32[2,32,128]{2,1,0:T(8,128)S(1)}, f32[2,32,128]{2,1,0:T(8,128)S(1)}, u32[]{:S(2)}, u32[]{:S(2)}) collective-permute-start(f32[2,32,128]{2,1,0:T(8,128)S(1)} %get-tuple-element.30.far), channel_id=1, source_target_pairs={{1,2},{3,4},{5,6},{7,8},{9,10},{11,12},{13,14},{2,1},{4,3},{6,5},{... | collective-permute-start | bytes 98312 | tf_op jit(solution)/shard_map/ppermute | solution.py:340
  6.3 6.5 %collective-permute-start.1 = (f32[2,32,128]{2,1,0:T(8,128)S(1)}, f32[2,32,128]{2,1,0:T(8,128)S(1)}, u32[]{:S(2)}, u32[]{:S(2)}) collective-permute-start(f32[2,32,128]{2,1,0:T(8,128)S(1)} %get-tuple-element.31.near), channel_id=1, source_target_pairs={{0,1},{1,0},{2,3},{3,2},{4,5},{5,4},{6,7},{7,6},{8,9},{9,8},{10,11... | collective-permute-start | bytes 98312 | tf_op jit(solution)/shard_map/ppermute | solution.py:341
  10.3 2.4 %copy-start.2 = (f32[32,32,128]{2,1,0:T(8,128)S(1)}, f32[32,32,128]{2,1,0:T(8,128)}, u32[]{:S(2)}) copy-start(f32[32,32,128]{2,1,0:T(8,128)} %param.5) | copy-start | bytes 1572868

commit v4 on v3

--- a/solution.py
+++ b/solution.py
@@ -14,7 +14,7 @@
 N = 32
 L = 128
 ROWS = N * N
-ROW = 8
+ROW = 5
 LAST = L // 2 - 1
 MID = LAST // 2
 VMEM_LIMIT = 24 << 20
@@ -93,11 +93,8 @@
         return k1
 
     k0 = k[xp(0), :]
-    mx[3] = k0
     k1 = lax.fori_loop(1, N - 1, plane, plane(0, k0), unroll=5)
-    mx[4] = k1
     flows(N - 1, k1, pltpu.roll(k1, N - 1, 0), pltpu.roll(h[xp(N - 1), :], N - 1, 0))
-    my[3], my[4] = k[yp(0), :], k[yp(N - 1), :]
 
     for g in range(8):
         wzt[pl.ds(g, L, stride=8), :] = jnp.transpose(wz[pl.ds(g * L, L), :])
@@ -138,8 +135,8 @@
     sx, sy, sz = lax.fori_loop(
         1, N - 1, chains, ((wx[xp(0), :], one, one), (wy[yp(0), :], one, one), sz), unroll=3
     )
-    mx[0], mx[2], mx[1] = sx
-    my[0], my[2], my[1] = sy
+    close_segment(mx, sx, COEF_X * k[xp(0), :], COEF_X * k[xp(N - 1), :])
+    close_segment(my, sy, COEF_Y * k[yp(0), :], COEF_Y * k[yp(N - 1), :])
     lo, (b0, e0, w0), o1, hi, p0, p1 = sz
     lo = (1.0 + e0 + o1[0]) + even_cell(MID - 1, lo, w0)
     hi = (1.0 + p0[0] + p1[1]) + even_cell(MID + 2, hi, p0[2])
@@ -147,12 +144,32 @@
     iz[zp(MID), :] = 1.0 / lo
 
 
-def send_segment(out, m, s0, s1):
-    for at, value in enumerate((m[0], m[1], m[2], s0, s1, m[3], m[4])):
+def close_segment(m, state, half0, half1):
+    beta, c, a = state
+    inv0 = 1.0 / (half0 + beta + a)
+    wh, bh = half0 * inv0, beta * inv0
+    past = wh * beta
+    c = c + bh * a
+    inv1 = 1.0 / (past + half1 + c)
+    lh, uh = past * inv1, half1 * inv1
+    for at, value in enumerate((lh * half1, wh * a + lh * c, uh * c, wh, bh, inv0, lh, uh, inv1)):
+        m[at] = value
+
+
+def send_segment(out, shares, m, r, s):
+    s = s + m[4] * r
+    for at, value in enumerate((m[0], m[1], m[2], m[3] * r + m[6] * s, m[7] * s)):
         out[pl.ds(at, N, stride=ROW), :] = value
-
-
-def x_down_kernel(f, rc, bx, ex, ix, mx, far, near, far_in, near_in, out, s_out, g):
+    shares[0], shares[1] = m[5] * r, m[8] * s
+
+
+def end_cells(ends, shares, m):
+    before, after = ends[pl.ds(0, N, stride=2), :], ends[pl.ds(1, N, stride=2), :]
+    last = shares[1] + m[6] * before + m[7] * after
+    return shares[0] + m[3] * before + m[4] * last, last
+
+
+def x_down_kernel(f, rc, bx, ex, ix, mx, far, near, far_in, near_in, out, s_out, shares, g):
     g[...] = f[...] + rc[...]
     at_near, at_far = halo_planes()
     for at, mine, theirs in ((at_far, far, far_in), (at_near, near, near_in)):
@@ -167,10 +184,10 @@
     s, r = lax.fori_loop(
         1, N - 1, step, (g[xp(1), :], g[xp(0), :]), unroll=5
     )
-    send_segment(out, mx, r, s)
-
-
-def ends_kernel(chunk, coef, net, out):
+    send_segment(out, shares, mx, r, s)
+
+
+def ends_kernel(chunk, net, out):
     row = lax.broadcasted_iota(jnp.int32, (N, L), 0)
 
     def before(v, s):
@@ -179,13 +196,13 @@
     def after(v, s):
         return jnp.where(row < N - s, pltpu.roll(v, N - s, 0), 0.0)
 
-    inner, c0, c1, s0, s1, k0, k1 = (net[pl.ds(at, N, stride=ROW), :] for at in range(7))
-    w = link(coef, before(k1, chunk), k0)
-    inv0 = 1.0 / (w + inner + c0)
-    wh, bh = w * inv0, inner * inv0
-    beta = w * bh
-    ground = c1 + bh * c0 + after(wh * c0, chunk)
-    rhs = s1 + bh * s0 + after(wh * s0, chunk)
+    past, g0, g1, r0, r1 = (net[pl.ds(at, N, stride=ROW), :] for at in range(ROW))
+    final = row >= N - chunk
+    inv_final = 1.0 / (past + g1)
+    share = jnp.where(final, past * inv_final, 0.0)
+    beta = before(past, chunk)
+    ground = g0 + before(g1, chunk) + share * g1
+    rhs = r0 + before(r1, chunk) + share * r1
     s = chunk
     while s < N:
         nxt = after(beta, s)
@@ -196,13 +213,12 @@
         beta = beta * before(lh, s)
         s *= 2
     q = rhs / ground
-    out[pl.ds(0, N, stride=2), :] = s0 * inv0 + wh * before(q, chunk) + bh * q
-    out[pl.ds(1, N, stride=2), :] = q
-
-
-def x_up_kernel(ends, s_in, bx, ex, h, by, ey, iy, my, out, s_out, d):
-    first = ends[pl.ds(0, N, stride=2), :]
-    last = ends[pl.ds(1, N, stride=2), :]
+    out[pl.ds(0, N, stride=2), :] = q
+    out[pl.ds(1, N, stride=2), :] = jnp.where(final, (r1 + past * q) * inv_final, after(q, chunk))
+
+
+def x_up_kernel(ends, s_in, bx, ex, mx, shares, h, by, ey, iy, my, out, s_out, shares_y, d):
+    first, last = end_cells(ends, shares, mx)
     d[xp(N - 1), :] = last - 2.0 * h[xp(N - 1), :]
     d[xp(0), :] = first - 2.0 * h[xp(0), :]
 
@@ -220,12 +236,11 @@
         return d[yp(i + 1), :] + ey[xp(i), :] * s, r + by[xp(i), :] * s
 
     s, r = lax.fori_loop(1, N - 1, step, (d[yp(1), :], d[yp(0), :]), unroll=10)
-    send_segment(out, my, r, s)
-
-
-def final_kernel(ends, s_in, by, ey, zb, ze, zi, ez, iz, h, out, d, t, sems):
-    first = ends[pl.ds(0, N, stride=2), :]
-    last = ends[pl.ds(1, N, stride=2), :]
+    send_segment(out, shares_y, my, r, s)
+
+
+def final_kernel(ends, s_in, by, ey, my, shares, zb, ze, zi, ez, iz, h, out, d, t, sems):
+    first, last = end_cells(ends, shares, my)
     d[xp(N - 1), :] = last
     d[xp(0), :] = first
 
@@ -323,10 +338,10 @@
     )(*args)
 
 
-def line_ends(net, axis, coef):
+def line_ends(net, axis):
     chunk = N // lax.axis_size(axis)
-    got = lax.all_to_all(net.reshape(N, ROW, L), axis, 0, 0, tiled=True).reshape(NET)
-    (ends,) = call(functools.partial(ends_kernel, chunk, coef), [ENDS], got, flops=100000)
+    got = lax.all_to_all(net.reshape(N, 1, ROW * L), axis, 0, 0, tiled=True).reshape(NET)
+    (ends,) = call(functools.partial(ends_kernel, chunk), [ENDS], got, flops=100000)
     return lax.all_to_all(ends.reshape(N, 2, L), axis, 0, 0, tiled=True).reshape(ENDS)
 
 
@@ -341,22 +356,27 @@
     near_in = lax.ppermute(near, "gy", [(i, i ^ 1) for i in range(count)])
     f, bx, ex, ix, mx, by, ey, iy, my, *z = call(
         local_kernel,
-        [BLOCK] * 4 + [planes(5)] + [BLOCK] * 3 + [planes(5)] + [HALF] * 5,
+        [BLOCK] * 4 + [planes(9)] + [BLOCK] * 3 + [planes(9)] + [HALF] * 5,
         h, k,
         scratch=[BLOCK] * 4,
         flops=20000000,
     )
-    net, sx = call(
+    net, sx, shares = call(
         x_down_kernel,
-        [NET, BLOCK],
+        [NET, BLOCK, planes(2)],
         f, rc, bx, ex, ix, mx, far, near, far_in, near_in,
         scratch=[BLOCK],
     )
-    ends = line_ends(net, "gx", COEF_X)
-    net, sy = call(x_up_kernel, [NET, BLOCK], ends, sx, bx, ex, h, by, ey, iy, my, scratch=[BLOCK])
-    ends = line_ends(net, "gy", COEF_Y)
+    ends = line_ends(net, "gx")
+    net, sy, shares = call(
+        x_up_kernel,
+        [NET, BLOCK, planes(2)],
+        ends, sx, bx, ex, mx, shares, h, by, ey, iy, my,
+        scratch=[BLOCK],
+    )
+    ends = line_ends(net, "gy")
     (out,) = call(
-        final_kernel, [BLOCK], ends, sy, by, ey, *z, h, hbm_out=True, scratch=[BLOCK] * 2, sems=8
+        final_kernel, [BLOCK], ends, sy, by, ey, my, shares, *z, h, hbm_out=True, scratch=[BLOCK] * 2, sems=8
     )
     return out.reshape(water_head.shape)
 

time: 75.8 us -> 74.1 us (0.978)
  blocking collectives: 60.1 us -> 58.4 us
    all_to_all x2, blocking collectives: 37.8 us -> 36.7 us  [line_ends(): lax.all_to_all(net.reshape(N, 1, ROW * L), axis, 0, 0, tiled=True)]
where the time goes in v4:
time: 74.1 us; the launch traced here: 73.8 us
  blocking collectives  58.4 us (79%)
  starting transfers between devices  9.41 us (13%)
  Pallas kernels  5.88 us (8%)
    all_to_all x2, blocking collectives, line_ends(): lax.all_to_all(net.reshape(N, 1, ROW * L), axis, 0, 0, tiled=True)  36.7 us
    all_to_all x2, blocking collectives, line_ends(): lax.all_to_all(ends.reshape(N, 2, L), axis, 0, 0, tiled=True).reshape(ENDS)  21.7 us
    pallas_call x7, Pallas kernels, call(): pl.pallas_call(kernel, out_shape=[make(s, jnp.float32) for s in outs], in...  5.88 us
    ppermute x1, starting transfers between devices, per_device(): far_in = lax.ppermute(far, 'gy', across + [(i, j) for j, i in across])  5.38 us
    ppermute x1, starting transfers between devices, per_device(): near_in = lax.ppermute(near, 'gy', [(i, i ^ 1) for i in range(count)])  4.03 us
  transfers between devices with their start and end apart: 2, of which 0 were waited for; matrix products, arithmetic and copies ran while one was open for 0% of the time, Pallas kernels for 3%

profile of v4, /device:TPU:1, one launch (start us, length us, event | category | flops | bytes accessed | tf_op | source)
XLA Modules:
  0.0 73.8 jit_solution(5908879727917727282)
XLA Ops:
  0.0 0.0 copy-start.1
  0.0 0.0 copy-start
  0.0 0.9 %shard_map.38 = (f32[2,32,128]{2,1,0:T(8,128)S(1)}, f32[2,32,128]{2,1,0:T(8,128)S(1)}) custom-call(f32[32,32,128]{2,1,0:T(8,128)} %h.1, f32[32,32,128]{2,1,0:T(8,128)} %k.1), custom_call_target="tpu_custom_call" | custom-call | flops 10000 | bytes 1048576 | tf_op jit(solution)/shard_map/pallas_call | solution.py:330
  0.9 5.4 %collective-permute-start = (f32[2,32,128]{2,1,0:T(8,128)S(1)}, f32[2,32,128]{2,1,0:T(8,128)S(1)}, u32[]{:S(2)}, u32[]{:S(2)}) collective-permute-start(f32[2,32,128]{2,1,0:T(8,128)S(1)} %get-tuple-element.32.far), channel_id=1, source_target_pairs={{1,2},{3,4},{5,6},{7,8},{9,10},{11,12},{13,14},{2,1},{4,3},{6,5},{... | collective-permute-start | bytes 98312 | tf_op jit(solution)/shard_map/ppermute | solution.py:355
  6.3 4.0 %collective-permute-start.1 = (f32[2,32,128]{2,1,0:T(8,128)S(1)}, f32[2,32,128]{2,1,0:T(8,128)S(1)}, u32[]{:S(2)}, u32[]{:S(2)}) collective-permute-start(f32[2,32,128]{2,1,0:T(8,128)S(1)} %get-tuple-element.33.near), channel_id=1, source_target_pairs={{0,1},{1,0},{2,3},{3,2},{4,5},{5,4},{6,7},{7,6},{8,9},{9,8},{10,11... | collective-permute-start | bytes 98312 | tf_op jit(solution)/shard_map/ppermute | solution.py:356
  10.3 0.0 copy-done.1
  10.3 0.0 copy-done
  10.3 0.0 copy-start.2
  10.4 2.4 %shard_map.37 = (f32[1024,128]{1,0:T(8,128)S(1)}, f32[1024,128]{1,0:T(8,128)S(1)}, f32[1024,128]{1,0:T(8,128)S(1)}, f32[1024,128]{1,0:T(8,128)S(1)}, f32[9,32,12...) custom-call(f32[1024,128]{1,0:T(8,128)S(1)} %bitcast.12, ...), custom_call_target="tpu_custom_call" | custom-call | flops 20000000 | bytes 1048576 | tf_op jit(solution)/shard_map/pallas_call | solution.py:330
  12.8 0.0 collective-permute-done.far_in
  12.8 0.0 collective-permute-done.1.near_in
  12.8 0.0 copy-done.2
  12.8 0.2 shard_map.39
  13.0 16.3 %all_to_all.20 = f32[32,1,640]{2,1,0:T(1,128)S(1)} all-to-all(f32[32,1,640]{2,1,0:T(1,128)S(1)} %bitcast.24), channel_id=1, replica_groups=mesh['gx'=32,'gy'=16] {'gx'}, dimensions={0} | all-to-all | bytes 163840 | tf_op jit(solution)/shard_map/all_to_all | solution.py:343
  29.4 0.1 shard_map.40
  29.5 11.9 %all_to_all.21 = f32[32,2,128]{2,1,0:T(2,128)S(1)} all-to-all(f32[32,2,128]{2,1,0:T(2,128)S(1)} %bitcast.21), channel_id=1, replica_groups=mesh['gx'=32,'gy'=16] {'gx'}, dimensions={0} | all-to-all | bytes 65536 | tf_op jit(solution)/shard_map/all_to_all | solution.py:345
  41.3 0.6 shard_map.41
  41.9 20.4 %all_to_all.22 = f32[32,1,640]{2,1,0:T(1,128)S(1)} all-to-all(f32[32,1,640]{2,1,0:T(1,128)S(1)} %bitcast.23), channel_id=1, replica_groups=mesh['gx'=32,'gy'=16] {'gy'}, dimensions={0} | all-to-all | bytes 163840 | tf_op jit(solution)/shard_map/all_to_all | solution.py:343
  62.3 0.1 shard_map.42
  62.4 9.9 %all_to_all.23 = f32[32,2,128]{2,1,0:T(2,128)S(1)} all-to-all(f32[32,2,128]{2,1,0:T(2,128)S(1)} %bitcast.22), channel_id=1, replica_groups=mesh['gx'=32,'gy'=16] {'gy'}, dimensions={0} | all-to-all | bytes 65536 | tf_op jit(solution)/shard_map/all_to_all | solution.py:345
  72.2 1.6 %shard_map.43 = f32[1024,128]{1,0:T(8,128)} custom-call(f32[64,128]{1,0:T(8,128)S(1)} %bitcast.19, f32[1024,128]{1,0:T(8,128)S(1)} %get-tuple-element.42.s_in, f32[1024,128]{1,0:T(8,128)S(1)} %get-tuple-element.37.by, f32[1024,128]{1,0:T(8,128)S(1)} %get-tuple-element.38.ey, f32[9,32,128]{2,1,0:T(8,128)S(1)} %get-tuple-element.40.my, ...), custom_call_target="tpu_custom_call" | custom-call | flops 1000000 | bytes 3620864 | tf_op jit(solution)/shard_map/pallas_call | solution.py:330
Async XLA Ops:
  0.0 10.3 %copy-start.1 = (f32[32,32,128]{2,1,0:T(8,128)S(1)}, f32[32,32,128]{2,1,0:T(8,128)}, u32[]{:S(2)}) copy-start(f32[32,32,128]{2,1,0:T(8,128)} %k.1) | copy-start | bytes 1572868
  0.0 10.3 %copy-start = (f32[32,32,128]{2,1,0:T(8,128)S(1)}, f32[32,32,128]{2,1,0:T(8,128)}, u32[]{:S(2)}) copy-start(f32[32,32,128]{2,1,0:T(8,128)} %h.1) | copy-start | bytes 1572868
  0.9 11.9 %collective-permute-start = (f32[2,32,128]{2,1,0:T(8,128)S(1)}, f32[2,32,128]{2,1,0:T(8,128)S(1)}, u32[]{:S(2)}, u32[]{:S(2)}) collective-permute-start(f32[2,32,128]{2,1,0:T(8,128)S(1)} %get-tuple-element.32.far), channel_id=1, source_target_pairs={{1,2},{3,4},{5,6},{7,8},{9,10},{11,12},{13,14},{2,1},{4,3},{6,5},{... | collective-permute-start | bytes 98312 | tf_op jit(solution)/shard_map/ppermute | solution.py:355
  6.3 6.5 %collective-permute-start.1 = (f32[2,32,128]{2,1,0:T(8,128)S(1)}, f32[2,32,128]{2,1,0:T(8,128)S(1)}, u32[]{:S(2)}, u32[]{:S(2)}) collective-permute-start(f32[2,32,128]{2,1,0:T(8,128)S(1)} %get-tuple-element.33.near), channel_id=1, source_target_pairs={{0,1},{1,0},{2,3},{3,2},{4,5},{5,4},{6,7},{7,6},{8,9},{9,8},{10,11... | collective-permute-start | bytes 98312 | tf_op jit(solution)/shard_map/ppermute | solution.py:356
  10.3 2.4 %copy-start.2 = (f32[32,32,128]{2,1,0:T(8,128)S(1)}, f32[32,32,128]{2,1,0:T(8,128)}, u32[]{:S(2)}) copy-start(f32[32,32,128]{2,1,0:T(8,128)} %param.5) | copy-start | bytes 1572868

commit v5 on v4

--- a/solution.py
+++ b/solution.py
@@ -300,8 +300,10 @@
     for g in range(8):
         at = pl.ds(g * L, L)
         d[at, :] = h[at, :] + jnp.transpose(t[pl.ds(g, L, stride=8), :])
-        copies.append(pltpu.make_async_copy(d.at[at, :], out.at[at, :], sems.at[g]))
-        copies[g].start()
+        for half in range(2):
+            part = pl.ds(g * L + half * (L // 2), L // 2)
+            copies.append(pltpu.make_async_copy(d.at[part, :], out.at[part, :], sems.at[2 * g + half]))
+            copies[-1].start()
     for copy in copies:
         copy.wait()
 
@@ -376,7 +378,7 @@
     )
     ends = line_ends(net, "gy")
     (out,) = call(
-        final_kernel, [BLOCK], ends, sy, by, ey, my, shares, *z, h, hbm_out=True, scratch=[BLOCK] * 2, sems=8
+        final_kernel, [BLOCK], ends, sy, by, ey, my, shares, *z, h, hbm_out=True, scratch=[BLOCK] * 2, sems=16
     )
     return out.reshape(water_head.shape)
 

time: 74.1 us -> 74.2 us (level)
  no operation moved by 1% of the time
where the time goes in v5:
time: 74.2 us; the launch traced here: 73.9 us
  blocking collectives  58.4 us (79%)
  starting transfers between devices  9.41 us (13%)
  Pallas kernels  5.94 us (8%)
    all_to_all x2, blocking collectives, line_ends(): lax.all_to_all(net.reshape(N, 1, ROW * L), axis, 0, 0, tiled=True)  36.7 us
    all_to_all x2, blocking collectives, line_ends(): lax.all_to_all(ends.reshape(N, 2, L), axis, 0, 0, tiled=True).reshape(ENDS)  21.7 us
    pallas_call x7, Pallas kernels, call(): pl.pallas_call(kernel, out_shape=[make(s, jnp.float32) for s in outs], in...  5.94 us
    ppermute x1, starting transfers between devices, per_device(): far_in = lax.ppermute(far, 'gy', across + [(i, j) for j, i in across])  5.38 us
    ppermute x1, starting transfers between devices, per_device(): near_in = lax.ppermute(near, 'gy', [(i, i ^ 1) for i in range(count)])  4.03 us
  transfers between devices with their start and end apart: 2, of which 0 were waited for; matrix products, arithmetic and copies ran while one was open for 0% of the time, Pallas kernels for 3%

profile of v5, /device:TPU:1, one launch (start us, length us, event | category | flops | bytes accessed | tf_op | source)
XLA Modules:
  0.0 73.9 jit_solution(7188233154498003178)
XLA Ops:
  0.0 0.0 copy-start.1
  0.0 0.0 copy-start
  0.0 0.9 %shard_map.38 = (f32[2,32,128]{2,1,0:T(8,128)S(1)}, f32[2,32,128]{2,1,0:T(8,128)S(1)}) custom-call(f32[32,32,128]{2,1,0:T(8,128)} %h.1, f32[32,32,128]{2,1,0:T(8,128)} %k.1), custom_call_target="tpu_custom_call" | custom-call | flops 10000 | bytes 1048576 | tf_op jit(solution)/shard_map/pallas_call | solution.py:332
  0.9 5.4 %collective-permute-start = (f32[2,32,128]{2,1,0:T(8,128)S(1)}, f32[2,32,128]{2,1,0:T(8,128)S(1)}, u32[]{:S(2)}, u32[]{:S(2)}) collective-permute-start(f32[2,32,128]{2,1,0:T(8,128)S(1)} %get-tuple-element.32.far), channel_id=1, source_target_pairs={{1,2},{3,4},{5,6},{7,8},{9,10},{11,12},{13,14},{2,1},{4,3},{6,5},{... | collective-permute-start | bytes 98312 | tf_op jit(solution)/shard_map/ppermute | solution.py:357
  6.3 4.0 %collective-permute-start.1 = (f32[2,32,128]{2,1,0:T(8,128)S(1)}, f32[2,32,128]{2,1,0:T(8,128)S(1)}, u32[]{:S(2)}, u32[]{:S(2)}) collective-permute-start(f32[2,32,128]{2,1,0:T(8,128)S(1)} %get-tuple-element.33.near), channel_id=1, source_target_pairs={{0,1},{1,0},{2,3},{3,2},{4,5},{5,4},{6,7},{7,6},{8,9},{9,8},{10,11... | collective-permute-start | bytes 98312 | tf_op jit(solution)/shard_map/ppermute | solution.py:358
  10.3 0.0 copy-done.1
  10.3 0.0 copy-done
  10.3 0.0 copy-start.2
  10.4 2.4 %shard_map.37 = (f32[1024,128]{1,0:T(8,128)S(1)}, f32[1024,128]{1,0:T(8,128)S(1)}, f32[1024,128]{1,0:T(8,128)S(1)}, f32[1024,128]{1,0:T(8,128)S(1)}, f32[9,32,12...) custom-call(f32[1024,128]{1,0:T(8,128)S(1)} %bitcast.12, ...), custom_call_target="tpu_custom_call" | custom-call | flops 20000000 | bytes 1048576 | tf_op jit(solution)/shard_map/pallas_call | solution.py:332
  12.8 0.0 collective-permute-done.far_in
  12.8 0.0 collective-permute-done.1.near_in
  12.8 0.0 copy-done.2
  12.8 0.2 shard_map.39
  13.0 16.3 %all_to_all.20 = f32[32,1,640]{2,1,0:T(1,128)S(1)} all-to-all(f32[32,1,640]{2,1,0:T(1,128)S(1)} %bitcast.24), channel_id=1, replica_groups=mesh['gx'=32,'gy'=16] {'gx'}, dimensions={0} | all-to-all | bytes 163840 | tf_op jit(solution)/shard_map/all_to_all | solution.py:345
  29.4 0.1 shard_map.40
  29.5 11.9 %all_to_all.21 = f32[32,2,128]{2,1,0:T(2,128)S(1)} all-to-all(f32[32,2,128]{2,1,0:T(2,128)S(1)} %bitcast.21), channel_id=1, replica_groups=mesh['gx'=32,'gy'=16] {'gx'}, dimensions={0} | all-to-all | bytes 65536 | tf_op jit(solution)/shard_map/all_to_all | solution.py:347
  41.3 0.6 shard_map.41
  41.9 20.4 %all_to_all.22 = f32[32,1,640]{2,1,0:T(1,128)S(1)} all-to-all(f32[32,1,640]{2,1,0:T(1,128)S(1)} %bitcast.23), channel_id=1, replica_groups=mesh['gx'=32,'gy'=16] {'gy'}, dimensions={0} | all-to-all | bytes 163840 | tf_op jit(solution)/shard_map/all_to_all | solution.py:345
  62.3 0.1 shard_map.42
  62.4 9.9 %all_to_all.23 = f32[32,2,128]{2,1,0:T(2,128)S(1)} all-to-all(f32[32,2,128]{2,1,0:T(2,128)S(1)} %bitcast.22), channel_id=1, replica_groups=mesh['gx'=32,'gy'=16] {'gy'}, dimensions={0} | all-to-all | bytes 65536 | tf_op jit(solution)/shard_map/all_to_all | solution.py:347
  72.2 1.7 %shard_map.43 = f32[1024,128]{1,0:T(8,128)} custom-call(f32[64,128]{1,0:T(8,128)S(1)} %bitcast.19, f32[1024,128]{1,0:T(8,128)S(1)} %get-tuple-element.42.s_in, f32[1024,128]{1,0:T(8,128)S(1)} %get-tuple-element.37.by, f32[1024,128]{1,0:T(8,128)S(1)} %get-tuple-element.38.ey, f32[9,32,128]{2,1,0:T(8,128)S(1)} %get-tuple-element.40.my, ...), custom_call_target="tpu_custom_call" | custom-call | flops 1000000 | bytes 3620864 | tf_op jit(solution)/shard_map/pallas_call | solution.py:332
Async XLA Ops:
  0.0 10.3 %copy-start.1 = (f32[32,32,128]{2,1,0:T(8,128)S(1)}, f32[32,32,128]{2,1,0:T(8,128)}, u32[]{:S(2)}) copy-start(f32[32,32,128]{2,1,0:T(8,128)} %k.1) | copy-start | bytes 1572868
  0.0 10.3 %copy-start = (f32[32,32,128]{2,1,0:T(8,128)S(1)}, f32[32,32,128]{2,1,0:T(8,128)}, u32[]{:S(2)}) copy-start(f32[32,32,128]{2,1,0:T(8,128)} %h.1) | copy-start | bytes 1572868
  0.9 11.9 %collective-permute-start = (f32[2,32,128]{2,1,0:T(8,128)S(1)}, f32[2,32,128]{2,1,0:T(8,128)S(1)}, u32[]{:S(2)}, u32[]{:S(2)}) collective-permute-start(f32[2,32,128]{2,1,0:T(8,128)S(1)} %get-tuple-element.32.far), channel_id=1, source_target_pairs={{1,2},{3,4},{5,6},{7,8},{9,10},{11,12},{13,14},{2,1},{4,3},{6,5},{... | collective-permute-start | bytes 98312 | tf_op jit(solution)/shard_map/ppermute | solution.py:357
  6.3 6.5 %collective-permute-start.1 = (f32[2,32,128]{2,1,0:T(8,128)S(1)}, f32[2,32,128]{2,1,0:T(8,128)S(1)}, u32[]{:S(2)}, u32[]{:S(2)}) collective-permute-start(f32[2,32,128]{2,1,0:T(8,128)S(1)} %get-tuple-element.33.near), channel_id=1, source_target_pairs={{0,1},{1,0},{2,3},{3,2},{4,5},{5,4},{6,7},{7,6},{8,9},{9,8},{10,11... | collective-permute-start | bytes 98312 | tf_op jit(solution)/shard_map/ppermute | solution.py:358
  10.3 2.4 %copy-start.2 = (f32[32,32,128]{2,1,0:T(8,128)S(1)}, f32[32,32,128]{2,1,0:T(8,128)}, u32[]{:S(2)}) copy-start(f32[32,32,128]{2,1,0:T(8,128)} %param.5) | copy-start | bytes 1572868

commit v6 on v5

--- a/solution.py
+++ b/solution.py
@@ -300,9 +300,9 @@
     for g in range(8):
         at = pl.ds(g * L, L)
         d[at, :] = h[at, :] + jnp.transpose(t[pl.ds(g, L, stride=8), :])
-        for half in range(2):
-            part = pl.ds(g * L + half * (L // 2), L // 2)
-            copies.append(pltpu.make_async_copy(d.at[part, :], out.at[part, :], sems.at[2 * g + half]))
+        if g % 2:
+            part = pl.ds((g - 1) * L, 2 * L)
+            copies.append(pltpu.make_async_copy(d.at[part, :], out.at[part, :], sems.at[g // 2]))
             copies[-1].start()
     for copy in copies:
         copy.wait()
@@ -378,7 +378,7 @@
     )
     ends = line_ends(net, "gy")
     (out,) = call(
-        final_kernel, [BLOCK], ends, sy, by, ey, my, shares, *z, h, hbm_out=True, scratch=[BLOCK] * 2, sems=16
+        final_kernel, [BLOCK], ends, sy, by, ey, my, shares, *z, h, hbm_out=True, scratch=[BLOCK] * 2, sems=4
     )
     return out.reshape(water_head.shape)
 

time: 74.2 us -> 74.1 us (level)
  no operation moved by 1% of the time
where the time goes in v6:
time: 74.1 us; the launch traced here: 73.8 us
  blocking collectives  58.4 us (79%)
  starting transfers between devices  9.41 us (13%)
  Pallas kernels  5.85 us (8%)
    all_to_all x2, blocking collectives, line_ends(): lax.all_to_all(net.reshape(N, 1, ROW * L), axis, 0, 0, tiled=True)  36.7 us
    all_to_all x2, blocking collectives, line_ends(): lax.all_to_all(ends.reshape(N, 2, L), axis, 0, 0, tiled=True).reshape(ENDS)  21.7 us
    pallas_call x7, Pallas kernels, call(): pl.pallas_call(kernel, out_shape=[make(s, jnp.float32) for s in outs], in...  5.85 us
    ppermute x1, starting transfers between devices, per_device(): far_in = lax.ppermute(far, 'gy', across + [(i, j) for j, i in across])  5.38 us
    ppermute x1, starting transfers between devices, per_device(): near_in = lax.ppermute(near, 'gy', [(i, i ^ 1) for i in range(count)])  4.03 us
  transfers between devices with their start and end apart: 2, of which 0 were waited for; matrix products, arithmetic and copies ran while one was open for 0% of the time, Pallas kernels for 3%

profile of v6, /device:TPU:1, one launch (start us, length us, event | category | flops | bytes accessed | tf_op | source)
XLA Modules:
  0.0 73.8 jit_solution(16439395388125696369)
XLA Ops:
  0.0 0.0 copy-start.1
  0.0 0.0 copy-start
  0.0 0.9 %shard_map.38 = (f32[2,32,128]{2,1,0:T(8,128)S(1)}, f32[2,32,128]{2,1,0:T(8,128)S(1)}) custom-call(f32[32,32,128]{2,1,0:T(8,128)} %h.1, f32[32,32,128]{2,1,0:T(8,128)} %k.1), custom_call_target="tpu_custom_call" | custom-call | flops 10000 | bytes 1048576 | tf_op jit(solution)/shard_map/pallas_call | solution.py:332
  0.9 5.4 %collective-permute-start = (f32[2,32,128]{2,1,0:T(8,128)S(1)}, f32[2,32,128]{2,1,0:T(8,128)S(1)}, u32[]{:S(2)}, u32[]{:S(2)}) collective-permute-start(f32[2,32,128]{2,1,0:T(8,128)S(1)} %get-tuple-element.32.far), channel_id=1, source_target_pairs={{1,2},{3,4},{5,6},{7,8},{9,10},{11,12},{13,14},{2,1},{4,3},{6,5},{... | collective-permute-start | bytes 98312 | tf_op jit(solution)/shard_map/ppermute | solution.py:357
  6.3 4.0 %collective-permute-start.1 = (f32[2,32,128]{2,1,0:T(8,128)S(1)}, f32[2,32,128]{2,1,0:T(8,128)S(1)}, u32[]{:S(2)}, u32[]{:S(2)}) collective-permute-start(f32[2,32,128]{2,1,0:T(8,128)S(1)} %get-tuple-element.33.near), channel_id=1, source_target_pairs={{0,1},{1,0},{2,3},{3,2},{4,5},{5,4},{6,7},{7,6},{8,9},{9,8},{10,11... | collective-permute-start | bytes 98312 | tf_op jit(solution)/shard_map/ppermute | solution.py:358
  10.3 0.0 copy-done.1
  10.3 0.0 copy-done
  10.3 0.0 copy-start.2
  10.4 2.4 %shard_map.37 = (f32[1024,128]{1,0:T(8,128)S(1)}, f32[1024,128]{1,0:T(8,128)S(1)}, f32[1024,128]{1,0:T(8,128)S(1)}, f32[1024,128]{1,0:T(8,128)S(1)}, f32[9,32,12...) custom-call(f32[1024,128]{1,0:T(8,128)S(1)} %bitcast.12, ...), custom_call_target="tpu_custom_call" | custom-call | flops 20000000 | bytes 1048576 | tf_op jit(solution)/shard_map/pallas_call | solution.py:332
  12.8 0.0 collective-permute-done.far_in
  12.8 0.0 collective-permute-done.1.near_in
  12.8 0.0 copy-done.2
  12.8 0.2 shard_map.39
  13.0 16.3 %all_to_all.20 = f32[32,1,640]{2,1,0:T(1,128)S(1)} all-to-all(f32[32,1,640]{2,1,0:T(1,128)S(1)} %bitcast.24), channel_id=1, replica_groups=mesh['gx'=32,'gy'=16] {'gx'}, dimensions={0} | all-to-all | bytes 163840 | tf_op jit(solution)/shard_map/all_to_all | solution.py:345
  29.4 0.1 shard_map.40
  29.5 11.9 %all_to_all.21 = f32[32,2,128]{2,1,0:T(2,128)S(1)} all-to-all(f32[32,2,128]{2,1,0:T(2,128)S(1)} %bitcast.21), channel_id=1, replica_groups=mesh['gx'=32,'gy'=16] {'gx'}, dimensions={0} | all-to-all | bytes 65536 | tf_op jit(solution)/shard_map/all_to_all | solution.py:347
  41.3 0.6 shard_map.41
  41.9 20.4 %all_to_all.22 = f32[32,1,640]{2,1,0:T(1,128)S(1)} all-to-all(f32[32,1,640]{2,1,0:T(1,128)S(1)} %bitcast.23), channel_id=1, replica_groups=mesh['gx'=32,'gy'=16] {'gy'}, dimensions={0} | all-to-all | bytes 163840 | tf_op jit(solution)/shard_map/all_to_all | solution.py:345
  62.3 0.1 shard_map.42
  62.4 9.9 %all_to_all.23 = f32[32,2,128]{2,1,0:T(2,128)S(1)} all-to-all(f32[32,2,128]{2,1,0:T(2,128)S(1)} %bitcast.22), channel_id=1, replica_groups=mesh['gx'=32,'gy'=16] {'gy'}, dimensions={0} | all-to-all | bytes 65536 | tf_op jit(solution)/shard_map/all_to_all | solution.py:347
  72.2 1.6 %shard_map.43 = f32[1024,128]{1,0:T(8,128)} custom-call(f32[64,128]{1,0:T(8,128)S(1)} %bitcast.19, f32[1024,128]{1,0:T(8,128)S(1)} %get-tuple-element.42.s_in, f32[1024,128]{1,0:T(8,128)S(1)} %get-tuple-element.37.by, f32[1024,128]{1,0:T(8,128)S(1)} %get-tuple-element.38.ey, f32[9,32,128]{2,1,0:T(8,128)S(1)} %get-tuple-element.40.my, ...), custom_call_target="tpu_custom_call" | custom-call | flops 1000000 | bytes 3620864 | tf_op jit(solution)/shard_map/pallas_call | solution.py:332
Async XLA Ops:
  0.0 10.3 %copy-start.1 = (f32[32,32,128]{2,1,0:T(8,128)S(1)}, f32[32,32,128]{2,1,0:T(8,128)}, u32[]{:S(2)}) copy-start(f32[32,32,128]{2,1,0:T(8,128)} %k.1) | copy-start | bytes 1572868
  0.0 10.3 %copy-start = (f32[32,32,128]{2,1,0:T(8,128)S(1)}, f32[32,32,128]{2,1,0:T(8,128)}, u32[]{:S(2)}) copy-start(f32[32,32,128]{2,1,0:T(8,128)} %h.1) | copy-start | bytes 1572868
  0.9 11.9 %collective-permute-start = (f32[2,32,128]{2,1,0:T(8,128)S(1)}, f32[2,32,128]{2,1,0:T(8,128)S(1)}, u32[]{:S(2)}, u32[]{:S(2)}) collective-permute-start(f32[2,32,128]{2,1,0:T(8,128)S(1)} %get-tuple-element.32.far), channel_id=1, source_target_pairs={{1,2},{3,4},{5,6},{7,8},{9,10},{11,12},{13,14},{2,1},{4,3},{6,5},{... | collective-permute-start | bytes 98312 | tf_op jit(solution)/shard_map/ppermute | solution.py:357
  6.3 6.5 %collective-permute-start.1 = (f32[2,32,128]{2,1,0:T(8,128)S(1)}, f32[2,32,128]{2,1,0:T(8,128)S(1)}, u32[]{:S(2)}, u32[]{:S(2)}) collective-permute-start(f32[2,32,128]{2,1,0:T(8,128)S(1)} %get-tuple-element.33.near), channel_id=1, source_target_pairs={{0,1},{1,0},{2,3},{3,2},{4,5},{5,4},{6,7},{7,6},{8,9},{9,8},{10,11... | collective-permute-start | bytes 98312 | tf_op jit(solution)/shard_map/ppermute | solution.py:358
  10.3 2.4 %copy-start.2 = (f32[32,32,128]{2,1,0:T(8,128)S(1)}, f32[32,32,128]{2,1,0:T(8,128)}, u32[]{:S(2)}) copy-start(f32[32,32,128]{2,1,0:T(8,128)} %param.5) | copy-start | bytes 1572868
